TPU v7x, 128 devices: a whole 4x4x4 slice. The times are simulated.
128 devices in a mesh: tm: 2 (over core), station: 16 (over y, x), channel: 4 (over z).
Axes of the slice: x: 4, y: 4, z: 4, core: 2. Of those that a mesh axis runs over, the one named last changes fastest.
Arguments:
- voltages: bfloat16 [2, 32, 2, 512, 512], P(None, 'channel', None, 'station', 'tm'), may hold values from -64 to 64
- start_seed: int32 [2, 32, 4, 2, 512], P(None, 'channel', None, None, 'station'), may hold values from -8 to 8
- beam_phase: int32 [512, 512], replicated, may hold values from 0 to 1023
- station_delay: int32 [512], replicated, may hold values from 0 to 1023
Outputs:
- beam_output: bfloat16 [2, 32, 2, 512, 512], P(None, 'channel', None, 'station', 'tm')
- subspace: float32 [2, 32, 4, 2, 512], P(None, 'channel', None, None, 'station')
All inputs are finite; a program needn't handle non-finite values.
Results may differ from a plain program's by a relative error of at most 0.017.
Values may be sent and summed in bfloat16 or wider, within the bound.
A program may use at most 64 MiB of HBM per device.

v0:
```python
import jax
import jax.numpy as jnp
from jax import lax
from jax.sharding import PartitionSpec as P

STATIONS = 512
CHANNELS = 32
ITERS = 3
PHASES = 1024


HIGH = lax.Precision.HIGHEST


def copy_for_each(value, axis):
    copies = jnp.broadcast_to(value, (lax.axis_size(axis), *value.shape))
    return lax.all_to_all(copies, axis, split_axis=0, concat_axis=0, tiled=True)


def of_everyone(value, axis):
    everything = copy_for_each(value, axis)
    return jnp.sum(everything.astype(jnp.float32), axis=0)


def of_everyone_2(value, axis):
    return copy_for_each(value, axis).sum(axis=0)


def coefficients(subspace, voltage):
    real_v = voltage[0].astype(jnp.float32)
    imag_v = voltage[1].astype(jnp.float32)
    pattern = "...kpm,...pmt->...kt"
    real_sum = jnp.einsum(pattern, subspace[0], real_v, precision=HIGH) + jnp.einsum(
        pattern, subspace[1], imag_v, precision=HIGH
    )
    imag_sum = jnp.einsum(pattern, subspace[0], imag_v, precision=HIGH) - jnp.einsum(
        pattern, subspace[1], real_v, precision=HIGH
    )
    return jnp.stack([real_sum, imag_sum])


def applied(voltage, coefficient):
    real_v = voltage[0].astype(jnp.float32)
    imag_v = voltage[1].astype(jnp.float32)
    pattern = "...pmt,...kt->...kpm"
    real_sum = jnp.einsum(pattern, real_v, coefficient[0], precision=HIGH) + jnp.einsum(
        pattern, imag_v, coefficient[1], precision=HIGH
    )
    imag_sum = jnp.einsum(pattern, imag_v, coefficient[0], precision=HIGH) - jnp.einsum(
        pattern, real_v, coefficient[1], precision=HIGH
    )
    return jnp.stack([real_sum, imag_sum])


def gram_matrix(image_field):
    pattern = "...kpm,...lpm->...kl"
    real_sum = jnp.einsum(pattern, image_field[0], image_field[0], precision=HIGH) + jnp.einsum(
        pattern, image_field[1], image_field[1], precision=HIGH
    )
    imag_sum = jnp.einsum(pattern, image_field[0], image_field[1], precision=HIGH) - jnp.einsum(
        pattern, image_field[1], image_field[0], precision=HIGH
    )
    return jnp.stack([real_sum, imag_sum])


def inverse_factor(gram_real, gram_imag):
    rank_count = gram_real.shape[-1]
    nothing = jnp.zeros_like(gram_real[..., 0, 0])
    low_real = {}
    low_imag = {}
    for column in range(rank_count):
        diagonal = gram_real[..., column, column]
        for middle in range(column):
            diagonal = diagonal - low_real[column, middle] ** 2 - low_imag[column, middle] ** 2
        pivot_root = jnp.sqrt(diagonal)
        low_real[column, column] = pivot_root
        low_imag[column, column] = nothing
        for row_at in range(column + 1, rank_count):
            acc_real = gram_real[..., row_at, column]
            acc_imag = gram_imag[..., row_at, column]
            for middle in range(column):
                acc_real = acc_real - (
                    low_real[row_at, middle] * low_real[column, middle]
                    + low_imag[row_at, middle] * low_imag[column, middle]
                )
                acc_imag = acc_imag - (
                    low_imag[row_at, middle] * low_real[column, middle]
                    - low_real[row_at, middle] * low_imag[column, middle]
                )
            low_real[row_at, column] = acc_real / pivot_root
            low_imag[row_at, column] = acc_imag / pivot_root
    inv_real = {}
    inv_imag = {}
    for column in range(rank_count):
        inv_real[column, column] = 1.0 / low_real[column, column]
        inv_imag[column, column] = nothing
        for row_at in range(column + 1, rank_count):
            acc_real = nothing
            acc_imag = nothing
            for middle in range(column, row_at):
                acc_real = (
                    acc_real
                    + low_real[row_at, middle] * inv_real[middle, column]
                    - low_imag[row_at, middle] * inv_imag[middle, column]
                )
                acc_imag = (
                    acc_imag
                    + low_real[row_at, middle] * inv_imag[middle, column]
                    + low_imag[row_at, middle] * inv_real[middle, column]
                )
            inv_real[row_at, column] = -acc_real / low_real[row_at, row_at]
            inv_imag[row_at, column] = -acc_imag / low_real[row_at, row_at]
    real_rows = [
        jnp.stack(
            [inv_real.get((row_at, column), nothing) for column in range(rank_count)], axis=-1
        )
        for row_at in range(rank_count)
    ]
    imag_rows = [
        jnp.stack(
            [inv_imag.get((row_at, column), nothing) for column in range(rank_count)], axis=-1
        )
        for row_at in range(rank_count)
    ]
    return (jnp.stack(real_rows, axis=-2), jnp.stack(imag_rows, axis=-2))


def orthonormal(image_field, sums):
    inv_real, inv_imag = inverse_factor(sums[0], sums[1])
    pattern = "...lpm,...kl->...kpm"
    real_sum = jnp.einsum(pattern, image_field[0], inv_real, precision=HIGH) + jnp.einsum(
        pattern, image_field[1], inv_imag, precision=HIGH
    )
    imag_sum = jnp.einsum(pattern, image_field[1], inv_real, precision=HIGH) - jnp.einsum(
        pattern, image_field[0], inv_imag, precision=HIGH
    )
    return jnp.stack([real_sum, imag_sum])


def project_out(voltage, subspace, coefficient):
    pattern = "...kpm,...kt->...pmt"
    real_sum = jnp.einsum(pattern, subspace[0], coefficient[0], precision=HIGH) - jnp.einsum(
        pattern, subspace[1], coefficient[1], precision=HIGH
    )
    imag_sum = jnp.einsum(pattern, subspace[0], coefficient[1], precision=HIGH) + jnp.einsum(
        pattern, subspace[1], coefficient[0], precision=HIGH
    )
    return jnp.stack(
        [voltage[0].astype(jnp.float32) - real_sum, voltage[1].astype(jnp.float32) - imag_sum]
    )


def beam_weights(phase_rows, delays, channel_numbers):
    summed = phase_rows + delays[None, :]
    index = summed[None, :, :] * (channel_numbers[:, None, None] + 1) % PHASES
    angle = index.astype(jnp.float32) * (2.0 * jnp.pi / PHASES)
    norming = 1.0 / jnp.sqrt(jnp.float32(STATIONS))
    return (
        (jnp.cos(angle) * norming).astype(jnp.bfloat16),
        (-jnp.sin(angle) * norming).astype(jnp.bfloat16),
    )


def form_beams(real_w, imag_w, cleaned):
    pattern = "cbm,cpmt->cpbt"
    real_sum = jnp.einsum(
        pattern, real_w, cleaned[0], preferred_element_type=jnp.float32
    ) - jnp.einsum(pattern, imag_w, cleaned[1], preferred_element_type=jnp.float32)
    imag_sum = jnp.einsum(
        pattern, real_w, cleaned[1], preferred_element_type=jnp.float32
    ) + jnp.einsum(pattern, imag_w, cleaned[0], preferred_element_type=jnp.float32)
    return jnp.stack([real_sum, imag_sum])


def body(voltages, start_seed, beam_phase, station_delay):
    chan_count = voltages.shape[1]
    time_count = voltages.shape[4]
    first_channel = lax.axis_index("channel") * chan_count
    channel_numbers = jnp.arange(chan_count, dtype=jnp.int32) + first_channel
    subspace = start_seed.astype(jnp.float32)
    for iteration in range(ITERS):
        coefficient = of_everyone(
            coefficients(subspace, voltages).astype(jnp.bfloat16), "station"
        ).astype(jnp.float32)
        partial_value = applied(voltages, coefficient)
        summed = of_everyone_2(partial_value, "tm")
        sums = of_everyone_2(gram_matrix(summed), "station")
        subspace = orthonormal(summed, sums)
    coefficient = of_everyone(
        coefficients(subspace, voltages).astype(jnp.bfloat16), "station"
    ).astype(jnp.float32)
    cleaned = project_out(voltages, subspace, coefficient).astype(jnp.bfloat16)
    beam_count = beam_phase.shape[0] // lax.axis_size("station")
    first_beam = lax.axis_index("station") * beam_count
    phase_rows = lax.dynamic_slice_in_dim(beam_phase, first_beam, beam_count, 0)
    real_w, imag_w = beam_weights(phase_rows, station_delay, channel_numbers)
    beam_field = form_beams(real_w, imag_w, lax.all_gather(cleaned, "station", axis=3, tiled=True))
    power_part = jnp.sum(beam_field[0] ** 2 + beam_field[1] ** 2, axis=(0, 3))
    total_time = time_count * lax.axis_size("tm")
    beam_power = of_everyone_2(power_part, ("tm", "channel")) / (CHANNELS * total_time)
    rescale = lax.rsqrt(beam_power + 1e-06)
    beam_output = (beam_field * rescale[None, None, :, :, None]).astype(jnp.bfloat16)
    return (beam_output, subspace)


def solution(mesh):
    in_specs = (
        P(None, "channel", None, "station", "tm"),
        P(None, "channel", None, None, "station"),
        P(),
        P(),
    )
    out_specs = (
        P(None, "channel", None, "station", "tm"),
        P(None, "channel", None, None, "station"),
    )
    return jax.shard_map(body, mesh=mesh, in_specs=in_specs, out_specs=out_specs, check_vma=False)
```

profile of v0, /device:TPU:1, one launch (start us, length us, event | category | flops | bytes accessed | tf_op | source)
XLA Modules:
  0.0 253.7 jit_solution(3533559155889441939)
XLA Ops:
  7.2 0.9 copy_convert_fusion
  8.1 1.2 convolution_bitcast_fusion.13
  9.3 1.2 convolution_bitcast_fusion.15
  10.6 1.2 fusion.40
  11.8 1.2 fusion.41
  13.2 17.9 %all_to_all.55 = bf16[16,2,8,4,256]{4,2,3,1,0:T(8,128)(2,1)S(1)} all-to-all(bf16[16,2,8,4,256]{4,2,3,1,0:T(8,128)(2,1)S(1)} %broadcast_in_dim.37), channel_id=1, replica_groups=mesh['tm'=2,'station'=16,'channel'=4] {'station'}, dimensions={0} | all-to-all | bytes 1048576 | tf_op jit(solution)/shard_map/all_to_all | solution.py:17
  31.2 1.6 fusion.68
  32.7 1.6 fusion.86
  34.3 1.6 fusion.23
  35.9 1.6 fusion.22
  37.6 5.4 %all_to_all.56 = f32[2,1,4096]{2,1,0:T(1,128)S(1)} all-to-all(f32[2,1,4096]{2,1,0:T(1,128)S(1)} %reshape.4061), channel_id=1, replica_groups=mesh['tm'=2,'station'=16,'channel'=4] {'tm'}, dimensions={0} | all-to-all | bytes 65536 | tf_op jit(solution)/shard_map/all_to_all | solution.py:17
  45.5 0.9 reshape.4063
  46.4 3.5 %all-to-all-start.2 = ((f32[16,1,256]{2,1,0:T(1,128)}), f32[16,1,256]{2,1,0:T(1,128)S(1)}, u32[]{:S(2)}, u32[]{:S(2)}) async-start(f32[16,1,256]{2,1,0:T(1,128)} %reshape.4063), calls=%async_computation.2 | async-start | bytes 32768 | tf_op jit(solution)/shard_map/all_to_all | solution.py:17
  50.1 6.2 %all-to-all-done.2 = f32[16,1,256]{2,1,0:T(1,128)S(1)} async-done(((f32[16,1,256]{2,1,0:T(1,128)}), f32[16,1,256]{2,1,0:T(1,128)S(1)}, u32[]{:S(2)}, u32[]{:S(2)}) %all-to-all-start.2) | async-done | bytes 16416 | tf_op jit(solution)/shard_map/all_to_all | solution.py:17
  60.5 13.2 %all_to_all.57 = bf16[16,2,8,4,256]{4,2,3,1,0:T(8,128)(2,1)S(1)} all-to-all(bf16[16,2,8,4,256]{4,2,3,1,0:T(8,128)(2,1)S(1)} %broadcast_in_dim.40), channel_id=1, replica_groups=mesh['tm'=2,'station'=16,'channel'=4] {'station'}, dimensions={0} | all-to-all | bytes 1048576 | tf_op jit(solution)/shard_map/all_to_all | solution.py:17
  76.4 5.8 %all_to_all.58 = f32[2,1,4096]{2,1,0:T(1,128)S(1)} all-to-all(f32[2,1,4096]{2,1,0:T(1,128)S(1)} %reshape.4065), channel_id=1, replica_groups=mesh['tm'=2,'station'=16,'channel'=4] {'tm'}, dimensions={0} | all-to-all | bytes 65536 | tf_op jit(solution)/shard_map/all_to_all | solution.py:17
  84.5 9.1 %all_to_all.59 = f32[16,1,256]{2,1,0:T(1,128)S(1)} all-to-all(f32[16,1,256]{2,1,0:T(1,128)S(1)} %reshape.4067), channel_id=1, replica_groups=mesh['tm'=2,'station'=16,'channel'=4] {'station'}, dimensions={0} | all-to-all | bytes 32768 | tf_op jit(solution)/shard_map/all_to_all | solution.py:17
  97.8 13.1 %all_to_all.60 = bf16[16,2,8,4,256]{4,2,3,1,0:T(8,128)(2,1)S(1)} all-to-all(bf16[16,2,8,4,256]{4,2,3,1,0:T(8,128)(2,1)S(1)} %broadcast_in_dim.43), channel_id=1, replica_groups=mesh['tm'=2,'station'=16,'channel'=4] {'station'}, dimensions={0} | all-to-all | bytes 1048576 | tf_op jit(solution)/shard_map/all_to_all | solution.py:17
  113.6 5.9 %all_to_all.61 = f32[2,1,4096]{2,1,0:T(1,128)S(1)} all-to-all(f32[2,1,4096]{2,1,0:T(1,128)S(1)} %reshape.4069), channel_id=1, replica_groups=mesh['tm'=2,'station'=16,'channel'=4] {'tm'}, dimensions={0} | all-to-all | bytes 65536 | tf_op jit(solution)/shard_map/all_to_all | solution.py:17
  119.5 0.7 reduce.4
  121.8 9.1 %all_to_all.62 = f32[16,1,256]{2,1,0:T(1,128)S(1)} all-to-all(f32[16,1,256]{2,1,0:T(1,128)S(1)} %reshape.4071), channel_id=1, replica_groups=mesh['tm'=2,'station'=16,'channel'=4] {'station'}, dimensions={0} | all-to-all | bytes 32768 | tf_op jit(solution)/shard_map/all_to_all | solution.py:17
  135.0 13.1 %all_to_all.63 = bf16[16,2,8,4,256]{4,2,3,1,0:T(8,128)(2,1)S(1)} all-to-all(bf16[16,2,8,4,256]{4,2,3,1,0:T(8,128)(2,1)S(1)} %broadcast_in_dim.46), channel_id=1, replica_groups=mesh['tm'=2,'station'=16,'channel'=4] {'station'}, dimensions={0} | all-to-all | bytes 1048576 | tf_op jit(solution)/shard_map/all_to_all | solution.py:17
  150.9 0.8 pad_maximum_fusion
  151.8 0.9 dynamic-slice_add_fusion
  152.6 70.1 %all-gather.2.cloned.1.call-done = bf16[2,8,2,512,256]{4,3,2,1,0:T(8,128)(2,1)} async-done(((bf16[2,8,2,32,256]{4,3,2,1,0:T(8,128)(2,1)}), bf16[2,8,2,512,256]{4,3,2,1,0:T(8,128)(2,1)}) %all-gather.2.cloned.1.call-update) | async-done | bytes 8388624 | tf_op jit(solution)/shard_map/all_gather | solution.py:197
  222.8 4.1 %fusion = f32[8,2,256,32]{2,3,1,0:T(8,128)S(1)} fusion(bf16[2,8,2,512,256]{4,3,2,1,0:T(8,128)(2,1)} %all-gather.2.cloned.1.call-done, s32[8]{0:T(128)S(1)} %add_add_fusion, s32[32,512]{1,0:T(8,128)S(1)} %dynamic-slice_add_fusion), kind=kOutput, calls=%fused_computation.2 | convolution fusion | flops 136314880 | bytes 4784160 | tf_op jit(solution)/shard_map/cbm,cpmt->cpbt/dot_general | solution.py:166
  226.9 3.9 %fusion.1 = f32[8,2,256,32]{2,3,1,0:T(8,128)S(1)} fusion(bf16[2,8,2,512,256]{4,3,2,1,0:T(8,128)(2,1)} %all-gather.2.cloned.1.call-done, s32[8]{0:T(128)S(1)} %add_add_fusion, s32[32,512]{1,0:T(8,128)S(1)} %dynamic-slice_add_fusion), kind=kOutput, calls=%fused_computation.3 | convolution fusion | flops 136445952 | bytes 4784160 | tf_op jit(solution)/shard_map/cbm,cpmt->cpbt/dot_general | solution.py:171
  230.8 2.1 fusion.7
  233.0 2.3 fusion.53
  235.9 5.1 %all-to-all-start.10 = ((f32[8,2,32]{2,1,0:T(2,128)}), f32[8,2,32]{2,1,0:T(2,128)S(1)}, u32[]{:S(2)}, u32[]{:S(2)}) async-start(f32[8,2,32]{2,1,0:T(2,128)} %broadcast_in_dim.47), calls=%async_computation.10 | async-start | bytes 16384 | tf_op jit(solution)/shard_map/all_to_all | solution.py:17
  241.6 4.2 %all-to-all-done.10 = f32[8,2,32]{2,1,0:T(2,128)S(1)} async-done(((f32[8,2,32]{2,1,0:T(2,128)}), f32[8,2,32]{2,1,0:T(2,128)S(1)}, u32[]{:S(2)}, u32[]{:S(2)}) %all-to-all-start.10) | async-done | bytes 2080 | tf_op jit(solution)/shard_map/all_to_all | solution.py:17
  245.9 1.0 fusion.48
  (183 shorter events, 28.3 us)
Async XLA Ops:
  7.2 51.8 %copy-start = (bf16[2,8,2,32,256]{4,3,2,1,0:T(8,128)(2,1)S(1)}, bf16[2,8,2,32,256]{4,3,2,1,0:T(8,128)(2,1)}, u32[]{:S(2)}) copy-start(bf16[2,8,2,32,256]{4,3,2,1,0:T(8,128)(2,1)} %param.4) | copy-start | bytes 1572868
  46.4 9.9 %all-to-all-start.2 = ((f32[16,1,256]{2,1,0:T(1,128)}), f32[16,1,256]{2,1,0:T(1,128)S(1)}, u32[]{:S(2)}, u32[]{:S(2)}) async-start(f32[16,1,256]{2,1,0:T(1,128)} %reshape.4063), calls=%async_computation.2 | async-start | bytes 32768 | tf_op jit(solution)/shard_map/all_to_all | solution.py:17
  49.9 172.9 %all-gather.2.cloned.1.call-start = ((), (), s32[]{:S(2)}) async-start(), calls=%async_computation.11 | async-start | bytes 8912896 | tf_op jit(solution)/shard_map/all_gather | solution.py:197
  97.1 54.7 %copy-start.1 = (s32[512]{0:T(512)S(1)}, s32[512]{0:T(512)}, u32[]{:S(2)}) copy-start(s32[512]{0:T(512)} %param.7) | copy-start | bytes 6148
  222.8 8.1 %copy-start.2 = (bf16[2,8,2,512,256]{4,3,2,1,0:T(8,128)(2,1)S(1)}, bf16[2,8,2,512,256]{4,3,2,1,0:T(8,128)(2,1)}, u32[]{:S(2)}) copy-start(bf16[2,8,2,512,256]{4,3,2,1,0:T(8,128)(2,1)} %all-gather.2.cloned.1.call-done) | copy-start | bytes 25165828
  235.9 10.0 %all-to-all-start.10 = ((f32[8,2,32]{2,1,0:T(2,128)}), f32[8,2,32]{2,1,0:T(2,128)S(1)}, u32[]{:S(2)}, u32[]{:S(2)}) async-start(f32[8,2,32]{2,1,0:T(2,128)} %broadcast_in_dim.47), calls=%async_computation.10 | async-start | bytes 16384 | tf_op jit(solution)/shard_map/all_to_all | solution.py:17
Sparse Core Ops, SparseCore 0:
  151.9 70.8 all-gather.1
where the time goes:
time: 255 us; the launch traced here: 254 us
  blocking collectives  92.5 us (36%)
  waiting for transfers between devices  80.6 us (32%)
  matrix products  40 us (16%)
  between operations  14.9 us (6%)
  other arithmetic  9.26 us (4%)
  starting transfers between devices  8.63 us (3%)
  local copies, waits for them, and re-layouts  7.85 us (3%)
    all_to_all x9, blocking collectives, copy_for_each(): return lax.all_to_all(copies, axis, split_axis=0, concat_axis=0, tiled=True)  92.5 us
    all_gather x1, waiting for transfers between devices, body(): lax.all_gather(cleaned, 'station', axis=3, tiled=True)  70.1 us
    all_to_all x2, waiting for transfers between devices, copy_for_each(): return lax.all_to_all(copies, axis, split_axis=0, concat_axis=0, tiled=True)  10.4 us
    all_to_all x2, starting transfers between devices, copy_for_each(): return lax.all_to_all(copies, axis, split_axis=0, concat_axis=0, tiled=True)  8.59 us
  transfers between devices with their start and end apart: 3, of which 3 were waited for; matrix products, arithmetic and copies ran while one was open for 1% of the time, Pallas kernels for 0%

commit v1 on v0

v1 whole, which is shorter than its diff:
```python
import functools

import jax
import jax.numpy as jnp
from jax import lax
from jax.experimental import pallas as pl
from jax.experimental.pallas import tpu as pltpu
from jax.sharding import PartitionSpec as P

STATIONS = 512
CHANNELS = 32
ITERS = 3
PHASES = 1024
TIME = 512
RANK = 4
GROUP = 16
QUARTERS = 4

MESH = pl.DeviceIdType.MESH

COS_TERMS = (
    0.9999999998855527,
    -4.934802185863431,
    4.058711817242859,
    -1.3352602861671086,
    0.23532082553812417,
    -0.025785808775470303,
    0.0019043289643584185,
    -8.86909374720357e-05,
)
SIN_TERMS = (
    3.141592653568331,
    -5.167712777297557,
    2.5501639819324518,
    -0.599264064211247,
    0.0821440508162118,
    -0.007366486943808629,
    0.000461586777512204,
    -1.8944663042615234e-05,
)


def horner(terms, scale, v):
    total = jnp.full_like(v, terms[-1] * scale)
    for term in terms[-2::-1]:
        total = total * v + jnp.float32(term * scale)
    return total


def three_parts(value):
    high = value.astype(jnp.bfloat16)
    rest = value - high.astype(jnp.float32)
    middle = rest.astype(jnp.bfloat16)
    low = (rest - middle.astype(jnp.float32)).astype(jnp.bfloat16)
    return high, middle, low


def sum_of_three(rows):
    return rows[0:8] + (rows[8:16] + rows[16:24])


def half_swap(rows):
    return pltpu.roll(rows, 4, 0)


def kernel(
    volt,
    seed,
    phase,
    delay,
    out,
    sub,
    local_x,
    phases,
    field,
    first_out,
    first_in,
    image,
    weights,
    product,
    stage,
    power_out,
    power_in,
    power_two,
    basis_out,
    basis_in,
    arrived,
    result,
    local_sem,
    send_x,
    recv_x,
    send_first,
    recv_first,
    send_image,
    recv_image,
    send_basis,
    recv_basis,
    send_power,
    recv_power,
    send_two,
    recv_two,
    send_beam,
    recv_beam,
    out_sem,
):
    core = lax.axis_index("tm")
    me = lax.axis_index("station")
    plane = lax.axis_index("channel")
    mine = me // 2
    half = me % 2
    twin = me + 1 - 2 * half
    quarter = core * 2 + half

    def partner(step):
        row = (me // 4 + step // 4) % 4
        column = (me % 4 + step % 4) % 4
        return row * 4 + column

    def rows_of(station, size):
        return pl.ds(pl.multiple_of(station * size, size), size)

    def lanes_of(which):
        return pl.ds(pl.multiple_of(which * 128, 128), 128)

    load_x = pltpu.make_async_copy(volt, local_x, local_sem.at[0])
    load_x.start()
    load_phase = pltpu.make_async_copy(phase, phases, local_sem.at[1])
    load_phase.start()

    barrier = pltpu.get_barrier_semaphore()
    three = (
        {"tm": 1 - core},
        {"station": twin},
        {"tm": 1 - core, "station": twin},
    )
    seven = [{"tm": 1 - core}]
    for step in range(1, 4):
        other = (plane + step) % 4
        seven.append({"channel": other})
        seven.append({"tm": 1 - core, "channel": other})

    def greet(step, carry):
        pl.semaphore_signal(barrier, inc=1, device_id={"station": partner(step)}, device_id_type=MESH)
        return carry

    lax.fori_loop(1, GROUP, greet, 0)
    for peer in seven:
        pl.semaphore_signal(barrier, inc=1, device_id=peer, device_id_type=MESH)
    pl.semaphore_signal(barrier, inc=1, device_id=three[2], device_id_type=MESH)
    pl.semaphore_wait(barrier, GROUP - 1 + len(seven) + 1)

    def x_copy(step, part):
        peer = partner(step)
        return pltpu.make_async_remote_copy(
            src_ref=volt.at[part, peer // 2, :, :, lanes_of(peer % 2)],
            dst_ref=field.at[:, rows_of(me, 32), pl.ds(part * 128, 128)],
            send_sem=send_x.at[part, step],
            recv_sem=recv_x.at[part, me],
            device_id={"station": peer},
            device_id_type=MESH,
        )

    def x_start(step, carry):
        x_copy(step, 0).start()
        x_copy(step, 1).start()
        return carry

    lax.fori_loop(1, GROUP, x_start, 0)
    own_x = [
        pltpu.make_async_copy(
            volt.at[part, mine, :, :, lanes_of(half)],
            field.at[:, rows_of(me, 32), pl.ds(part * 128, 128)],
            local_sem.at[2 + part],
        )
        for part in range(2)
    ]
    for copy in own_x:
        copy.start()

    load_x.wait()
    for c in range(8):
        total = jnp.zeros((8, 256), jnp.float32)
        for p in range(2):
            real_s = seed[0, c, pl.ds(p, 4, stride=2), :].astype(jnp.float32)
            imag_s = seed[1, c, pl.ds(p, 4, stride=2), :].astype(jnp.float32)
            on_real = jnp.concatenate([real_s, -imag_s], axis=0).astype(jnp.bfloat16)
            on_imag = jnp.concatenate([imag_s, real_s], axis=0).astype(jnp.bfloat16)
            total += jnp.dot(on_real, local_x[0, c, p], preferred_element_type=jnp.float32)
            total += jnp.dot(on_imag, local_x[1, c, p], preferred_element_type=jnp.float32)
        first_out[2 * c] = total[:, 0:128]
        first_out[2 * c + 1] = total[:, 128:256]

    def first_copy(step):
        peer = partner(step)
        return pltpu.make_async_remote_copy(
            src_ref=first_out.at[peer],
            dst_ref=first_in.at[me],
            send_sem=send_first.at[step],
            recv_sem=recv_first.at[me],
            device_id={"station": peer},
            device_id_type=MESH,
        )

    def first_start(step, carry):
        first_copy(step).start()
        return carry

    lax.fori_loop(1, GROUP, first_start, 0)
    first_in[me] = first_out[me]

    load_phase.wait()
    number = plane * 8 + mine + 1
    norming = STATIONS**-0.5

    def weight_rows(block, carry):
        rows = rows_of(block, 32)
        index = (phases[rows, :] + delay[...]) * number
        wrapped = (index + PHASES // 2) & (PHASES - 1)
        u = (wrapped - PHASES // 2).astype(jnp.float32) * jnp.float32(2.0 / PHASES)
        v = u * u
        weights[0, rows, :] = horner(COS_TERMS, norming, v).astype(jnp.bfloat16)
        weights[1, rows, :] = (u * horner(SIN_TERMS, -norming, v)).astype(jnp.bfloat16)
        return carry

    lax.fori_loop(0, 16, weight_rows, 0)

    def arrive(step, carry):
        source = partner(step)
        for part in range(2):
            pltpu.make_async_remote_copy(
                src_ref=volt.at[part, mine, :, :, lanes_of(half)],
                dst_ref=field.at[:, rows_of(source, 32), pl.ds(part * 128, 128)],
                send_sem=send_x.at[part, step],
                recv_sem=recv_x.at[part, source],
                device_id={"station": source},
                device_id_type=MESH,
            ).wait_recv()
        pltpu.make_async_remote_copy(
            src_ref=first_out.at[source],
            dst_ref=first_in.at[source],
            send_sem=send_first.at[step],
            recv_sem=recv_first.at[source],
            device_id={"station": source},
            device_id_type=MESH,
        ).wait_recv()
        return carry

    lax.fori_loop(1, GROUP, arrive, 0)
    for copy in own_x:
        copy.wait()

    row = lax.broadcasted_iota(jnp.int32, (8, 128), 0)
    upper = jnp.where(row < 4, 1.0, -1.0).astype(jnp.float32)

    def turned(c8):
        return jnp.concatenate([c8, half_swap(c8) * upper], axis=1)

    def apply_field(c8):
        left = jnp.concatenate(three_parts(turned(c8)), axis=0)
        right = field[...].reshape(1024, 256)
        rows = lax.dot_general(left, right, (((1,), (1,)), ((), ())), preferred_element_type=jnp.float32)
        return sum_of_three(rows)

    def coefficients(h8):
        left = jnp.concatenate(three_parts(h8), axis=0)
        rows = jnp.dot(left, field[...].reshape(1024, 256), preferred_element_type=jnp.float32)
        rows = sum_of_three(rows)
        return rows[:, 0:128] - upper * half_swap(rows[:, 128:256])

    def factor(h8):
        shifted = []
        for shift in range(4):
            moved = h8 * (pltpu.roll(h8, shift, 0) if shift else h8)
            lanes = moved[:, 0:128]
            for block in range(1, 8):
                lanes = lanes + moved[:, block * 128 : (block + 1) * 128]
            dots = jnp.broadcast_to(jnp.sum(lanes, axis=1, keepdims=True), (8, 128))
            swapped = half_swap(dots)
            shifted.append((dots + swapped, dots - swapped))

        def pick(rows, at):
            return jnp.broadcast_to(rows[at : at + 1, :], (8, 128))

        low = {}
        inverse = {}
        for column in range(RANK):
            diagonal = pick(shifted[0][0], column)
            for middle in range(column):
                re, im = low[column, middle]
                diagonal = diagonal - (re * re + im * im)
            inverse[column] = lax.rsqrt(diagonal)
            for at in range(column + 1, RANK):
                distance = at - column
                re = pick(shifted[distance][0], at)
                im = pick(shifted[4 - distance][1], column)
                for middle in range(column):
                    a_re, a_im = low[at, middle]
                    b_re, b_im = low[column, middle]
                    re = re - (a_re * b_re + a_im * b_im)
                    im = im - (a_im * b_re - a_re * b_im)
                low[at, column] = (re * inverse[column], im * inverse[column])
        return low, inverse

    def solve(low, inverse, rows):
        width = rows.shape[1]
        repeat = width // 128

        def wide(value):
            return value if repeat == 1 else jnp.concatenate([value] * repeat, axis=1)

        done = []
        for at in range(RANK):
            re = jnp.broadcast_to(rows[at : at + 1, :], (8, width))
            im = jnp.broadcast_to(rows[at + 4 : at + 5, :], (8, width))
            for middle in range(at):
                l_re, l_im = low[at, middle]
                l_re, l_im = wide(l_re), wide(l_im)
                d_re, d_im = done[middle]
                re = re - (l_re * d_re - l_im * d_im)
                im = im - (l_re * d_im + l_im * d_re)
            scale = wide(inverse[at])
            done.append((re * scale, im * scale))
        at_row = lax.broadcasted_iota(jnp.int32, (8, width), 0)
        total = done[3][1]
        for at in range(RANK):
            total = jnp.where(at_row == at, done[at][0], total)
            if at < 3:
                total = jnp.where(at_row == at + 4, done[at][1], total)
        return total

    coefficient = first_in[0]
    for station in range(1, GROUP):
        coefficient = coefficient + first_in[station]

    image_copies = []
    for iteration in range(ITERS):
        image[iteration, quarter] = apply_field(coefficient)
        for at, peer in enumerate(three):
            copy = pltpu.make_async_remote_copy(
                src_ref=image.at[iteration, quarter],
                dst_ref=image.at[iteration, quarter],
                send_sem=send_image.at[iteration, at],
                recv_sem=recv_image.at[iteration, at],
                device_id=peer,
                device_id_type=MESH,
            )
            copy.start()
            image_copies.append(copy)
        for copy in image_copies[-3:]:
            copy.wait_recv()
        summed = (image[iteration, 0] + image[iteration, 1]) + (image[iteration, 2] + image[iteration, 3])
        raw = coefficients(summed)
        low, inverse = factor(summed)
        coefficient = solve(low, inverse, raw)
    basis = solve(low, inverse, summed)

    for p in range(2):
        for block in range(4):
            lanes = basis[:, p * 512 + block * 128 : p * 512 + (block + 1) * 128] * upper
            for inner in range(4):
                moved = pltpu.roll(lanes, 128 - 32 * inner, 1) if inner else lanes
                basis_out[block * 4 + inner, p * 8 : (p + 1) * 8, :] = moved

    def basis_copy(step, slot, peer):
        return pltpu.make_async_remote_copy(
            src_ref=basis_out.at[peer],
            dst_ref=basis_in.at[slot],
            send_sem=send_basis.at[step],
            recv_sem=recv_basis.at[slot],
            device_id={"station": peer},
            device_id_type=MESH,
        )

    def basis_start(step, carry):
        peer = partner(step)

        @pl.when(peer // 8 == half)
        def _():
            basis_copy(step, mine, peer).start()

        return carry

    def six(parts, which):
        return jnp.concatenate([parts[at] for at in which], axis=0)

    basis_parts = three_parts(basis)
    coefficient_parts = three_parts(turned(coefficient))
    left = six(basis_parts, (0, 0, 1, 0, 1, 2))
    right = six(coefficient_parts, (0, 1, 0, 2, 1, 0))
    removed = lax.dot_general(left, right, (((0,), (0,)), ((), ())), preferred_element_type=jnp.float32)
    cleaned = field[...].reshape(1024, 256).astype(jnp.float32) - removed
    cleaned = cleaned.astype(jnp.bfloat16)
    for p in range(2):
        ours = cleaned[p * 512 : (p + 1) * 512]
        on_real = jnp.dot(weights[0], ours, preferred_element_type=jnp.float32)
        on_imag = jnp.dot(weights[1], ours, preferred_element_type=jnp.float32)
        product[p, :, 0:128] = on_real[:, 0:128] - on_imag[:, 128:256]
        product[p, :, 128:256] = on_real[:, 128:256] + on_imag[:, 0:128]

    def beam_copy(step, peer):
        return pltpu.make_async_remote_copy(
            src_ref=stage.at[:, :, rows_of(peer, 32), :],
            dst_ref=arrived.at[:, mine, :, :, lanes_of(half)],
            send_sem=send_beam.at[step],
            recv_sem=recv_beam.at[me],
            device_id={"station": peer},
            device_id_type=MESH,
        )

    def power_copy(step, peer):
        return pltpu.make_async_remote_copy(
            src_ref=power_out.at[peer],
            dst_ref=power_in.at[me],
            send_sem=send_power.at[step],
            recv_sem=recv_power.at[me],
            device_id={"station": peer},
            device_id_type=MESH,
        )

    lane_group = lax.broadcasted_iota(jnp.int32, (8, 128), 1) // 16

    def finish_block(peer):
        rows = rows_of(peer, 32)
        compact = jnp.zeros((8, 128), jnp.float32)
        for p in range(2):
            real_b = product[p, rows, 0:128]
            imag_b = product[p, rows, 128:256]
            stage[0, p, rows, :] = real_b.astype(jnp.bfloat16)
            stage[1, p, rows, :] = imag_b.astype(jnp.bfloat16)
            squares = jnp.sum(real_b * real_b + imag_b * imag_b, axis=1, keepdims=True)
            for block in range(4):
                compact = jnp.where(
                    lane_group == p * 4 + block,
                    jnp.broadcast_to(squares[block * 8 : (block + 1) * 8], (8, 128)),
                    compact,
                )
        power_out[peer] = compact

    def beam_start(step, carry):
        peer = partner(step)
        finish_block(peer)
        power_copy(step, peer).start()
        beam_copy(step, peer).start()
        return carry

    lax.fori_loop(1, GROUP, beam_start, 0)
    finish_block(me)
    power_in[me] = power_out[me]
    own_beam = pltpu.make_async_copy(
        stage.at[:, :, rows_of(me, 32), :],
        arrived.at[:, mine, :, :, lanes_of(half)],
        local_sem.at[4],
    )
    own_beam.start()

    lax.fori_loop(1, GROUP, basis_start, 0)

    @pl.when(me // 8 == half)
    def _():
        basis_in[mine] = basis_out[me]

    def power_arrive(step, carry):
        source = partner(step)
        pltpu.make_async_remote_copy(
            src_ref=power_out.at[source],
            dst_ref=power_in.at[source],
            send_sem=send_power.at[step],
            recv_sem=recv_power.at[source],
            device_id={"station": source},
            device_id_type=MESH,
        ).wait_recv()
        return carry

    lax.fori_loop(1, GROUP, power_arrive, 0)
    power = power_in[0]
    for station in range(1, GROUP):
        power = power + power_in[station]
    slot = plane * 2 + core
    power_two[slot] = power
    two_copies = []
    for at, peer in enumerate(seven):
        copy = pltpu.make_async_remote_copy(
            src_ref=power_two.at[slot],
            dst_ref=power_two.at[slot],
            send_sem=send_two.at[at],
            recv_sem=recv_two.at[at],
            device_id=peer,
            device_id_type=MESH,
        )
        copy.start()
        two_copies.append(copy)
    for copy in two_copies:
        copy.wait_recv()
    power = power_two[0]
    for at in range(1, 8):
        power = power + power_two[at]
    rescale = lax.rsqrt(power / (CHANNELS * TIME) + 1e-06)

    for c in range(8):

        @pl.when(2 * c + me // 8 != me)
        def _():
            basis_copy(0, c, 2 * c + me // 8).wait_recv()

    for c in range(8):
        for p in range(2):
            for part in range(2):
                at = p * 8 + part * 4
                sub[part, c, pl.ds(p, 4, stride=2), :] = basis_in[c, at : at + 4, 0:32]

    def beam_arrive(step, carry):
        source = partner(step)
        pltpu.make_async_remote_copy(
            src_ref=stage.at[:, :, rows_of(me, 32), :],
            dst_ref=arrived.at[:, source // 2, :, :, lanes_of(source % 2)],
            send_sem=send_beam.at[step],
            recv_sem=recv_beam.at[source],
            device_id={"station": source},
            device_id_type=MESH,
        ).wait_recv()
        return carry

    lax.fori_loop(1, GROUP, beam_arrive, 0)
    own_beam.wait()

    scales = []
    for p in range(2):
        rows = []
        for block in range(4):
            lane = (p * 4 + block) * 16
            rows.append(jnp.broadcast_to(rescale[:, lane : lane + 1], (8, 256)))
        scales.append(jnp.concatenate(rows, axis=0))

    def out_copy(c):
        return pltpu.make_async_copy(result.at[:, c], out.at[:, c], out_sem.at[c])

    def normalise(c, carry):
        for part in range(2):
            for p in range(2):
                value = arrived[part, c, p].astype(jnp.float32) * scales[p]
                result[part, c, p] = value.astype(jnp.bfloat16)
        out_copy(c).start()
        return carry

    lax.fori_loop(0, 8, normalise, 0)

    def drain(step, carry):
        peer = partner(step)
        x_copy(step, 0).wait_send()
        x_copy(step, 1).wait_send()
        first_copy(step).wait_send()
        power_copy(step, peer).wait_send()
        beam_copy(step, peer).wait_send()

        @pl.when(peer // 8 == half)
        def _():
            basis_copy(step, mine, peer).wait_send()

        return carry

    lax.fori_loop(1, GROUP, drain, 0)
    for copy in image_copies + two_copies:
        copy.wait_send()

    def out_wait(c, carry):
        out_copy(c).wait()
        return carry

    lax.fori_loop(0, 8, out_wait, 0)


def body(voltages, start_seed, beam_phase, station_delay):
    vmem = pl.BlockSpec(memory_space=pltpu.VMEM)
    anywhere = pl.BlockSpec(memory_space=pl.ANY)
    dma = pltpu.SemaphoreType.DMA
    f32, bf16 = jnp.float32, jnp.bfloat16
    beam_output, subspace = pl.pallas_call(
        kernel,
        out_shape=(
            jax.ShapeDtypeStruct((2, 8, 2, 32, 256), bf16),
            jax.ShapeDtypeStruct((2, 8, 8, 32), f32),
        ),
        in_specs=[anywhere, vmem, anywhere, vmem],
        out_specs=(anywhere, vmem),
        scratch_shapes=[
            pltpu.VMEM((2, 8, 2, 32, 256), bf16),
            pltpu.VMEM((512, 512), jnp.int32),
            pltpu.VMEM((2, 512, 256), bf16),
            pltpu.VMEM((16, 8, 128), f32),
            pltpu.VMEM((16, 8, 128), f32),
            pltpu.VMEM((ITERS, QUARTERS, 8, 1024), f32),
            pltpu.VMEM((2, 512, 512), bf16),
            pltpu.VMEM((2, 512, 256), f32),
            pltpu.VMEM((2, 2, 512, 128), bf16),
            pltpu.VMEM((16, 8, 128), f32),
            pltpu.VMEM((16, 8, 128), f32),
            pltpu.VMEM((8, 8, 128), f32),
            pltpu.VMEM((16, 16, 128), f32),
            pltpu.VMEM((8, 16, 128), f32),
            pltpu.VMEM((2, 8, 2, 32, 256), bf16),
            pltpu.VMEM((2, 8, 2, 32, 256), bf16),
            dma((5,)),
            dma((2, 16)),
            dma((2, 16)),
            dma((16,)),
            dma((16,)),
            dma((ITERS, 3)),
            dma((ITERS, 3)),
            dma((16,)),
            dma((8,)),
            dma((16,)),
            dma((16,)),
            dma((7,)),
            dma((7,)),
            dma((16,)),
            dma((16,)),
            dma((8,)),
        ],
        compiler_params=pltpu.CompilerParams(
            collective_id=0, has_side_effects=True, vmem_limit_bytes=40 * 1024 * 1024
        ),
    )(
        voltages,
        start_seed.reshape(2, 8, 8, 32),
        beam_phase,
        station_delay.reshape(1, STATIONS),
    )
    return beam_output, subspace.reshape(2, 8, 4, 2, 32)


def solution(mesh):
    in_specs = (
        P(None, "channel", None, "station", "tm"),
        P(None, "channel", None, None, "station"),
        P(),
        P(),
    )
    out_specs = (
        P(None, "channel", None, "station", "tm"),
        P(None, "channel", None, None, "station"),
    )
    return jax.shard_map(body, mesh=mesh, in_specs=in_specs, out_specs=out_specs, check_vma=False)
```

time: 255 us -> 53 us (0.21)
  blocking collectives: 92.5 us -> 0 us
  waiting for transfers between devices: 80.6 us -> 0 us
  Pallas kernels: 0 us -> 46.9 us
  matrix products: 40 us -> 0 us
  between operations: 14.9 us -> 0.65 us
  other arithmetic: 9.26 us -> 0 us
  starting transfers between devices: 8.63 us -> 0 us
  local copies, waits for them, and re-layouts: 7.85 us -> 5.2 us
    all_to_all x9 -> x0, blocking collectives: 92.5 us -> none  [copy_for_each(): return lax.all_to_all(copies, axis, split_axis=0, concat_axis=0, tiled=True)]
    all_gather x1 -> x0, waiting for transfers between devices: 70.1 us -> none  [body(): lax.all_gather(cleaned, 'station', axis=3, tiled=True)]
    pallas_call x0 -> x1, Pallas kernels: none -> 46.9 us  [body(): pl.pallas_call(kernel, out_shape=(jax.ShapeDtypeStruct((2, 8, 2, 32, 256)...]
    dot_general x60 -> x0, matrix products: 40 us -> none  [the longest x1 4.15 us: form_beams(): jnp.einsum(pattern, real_w, cleaned[0], preferred_element_type=jnp.float32)]
    all_to_all x2 -> x0, waiting for transfers between devices: 10.4 us -> none  [copy_for_each(): return lax.all_to_all(copies, axis, split_axis=0, concat_axis=0, tiled=True)]
    all_to_all x2 -> x0, starting transfers between devices: 8.59 us -> none  [copy_for_each(): return lax.all_to_all(copies, axis, split_axis=0, concat_axis=0, tiled=True)]
    all_to_all x6 -> x0, other arithmetic: 4.25 us -> none  [copy_for_each(): return lax.all_to_all(copies, axis, split_axis=0, concat_axis=0, tiled=True)]
    unnamed x25 -> x10, local copies, waits for them, and re-layouts: 3.95 us -> 5.2 us
  transfers between devices with their start and end apart: 3 -> 0, of which waited for: 3 -> 0; matrix products, arithmetic and copies ran while one was open for 1% -> 0% of each run, Pallas kernels for 0% -> 0%
where the time goes in v1:
time: 53 us; the launch traced here: 52.8 us
  Pallas kernels  46.9 us (88%)
  local copies, waits for them, and re-layouts  5.2 us (10%)
  between operations  0.65 us (1%)
    pallas_call x1, Pallas kernels, body(): pl.pallas_call(kernel, out_shape=(jax.ShapeDtypeStruct((2, 8, 2, 32, 256)...  46.9 us
    unnamed x10, local copies, waits for them, and re-layouts  5.2 us

profile of v1, /device:TPU:1, one launch (start us, length us, event | category | flops | bytes accessed | tf_op | source)
XLA Modules:
  0.0 52.8 jit_solution(12184084510198977957)
XLA Ops:
  0.6 0.0 copy-start.3
  0.6 0.7 %copy-done.3 = s32[512]{0:T(512)S(1)} copy-done((s32[512]{0:T(512)S(1)}, s32[512]{0:T(512)}, u32[]{:S(2)}) %copy-start.3) | copy-done | bytes 2072
  1.3 0.0 copy-start
  1.3 1.2 %copy-done = s32[512,512]{1,0:T(8,128)S(1)} copy-done((s32[512,512]{1,0:T(8,128)S(1)}, s32[512,512]{1,0:T(8,128)}, u32[]{:S(2)}) %copy-start) | copy-done | bytes 1048600
  2.5 0.0 copy-start.1
  2.5 1.0 %copy-done.1 = bf16[2,8,2,32,256]{4,3,2,1,0:T(8,128)(2,1)S(1)} copy-done((bf16[2,8,2,32,256]{4,3,2,1,0:T(8,128)(2,1)S(1)}, bf16[2,8,2,32,256]{4,3,2,1,0:T(8,128)(2,1)}, u32[]{:S(2)}) %copy-start.1) | copy-done | bytes 524312
  3.6 0.0 copy-start.2
  3.6 0.8 %copy-done.2 = s32[2,8,4,2,32]{4,3,2,1,0:T(2,128)S(1)} copy-done((s32[2,8,4,2,32]{4,3,2,1,0:T(2,128)S(1)}, s32[2,8,4,2,32]{4,3,2,1,0:T(2,128)}, u32[]{:S(2)}) %copy-start.2) | copy-done | bytes 16408
  4.4 46.9 %shard_map.59 = (bf16[2,8,2,32,256]{4,3,2,1,0:T(8,128)(2,1)S(1)}, f32[2,8,8,32]{3,2,1,0:T(8,128)S(1)}) custom-call(bf16[2,8,2,32,256]{4,3,2,1,0:T(8,128)(2,1)S(1)} %copy-done.1, s32[2,8,8,32]{3,2,1,0:T(8,128)S(1)} %bitcast.3, s32[512,512]{1,0:T(8,128)S(1)} %copy-done, s32[1,512]{1,0:T(1,128)S(1)} %bitcast.5), custom_call_target="tpu_custom_call" | custom-call | tf_op jit(solution)/shard_map/pallas_call | solution.py:577
  51.3 0.8 %copy.8 = bf16[2,8,2,32,256]{4,3,2,1,0:T(8,128)(2,1)} copy(bf16[2,8,2,32,256]{4,3,2,1,0:T(8,128)(2,1)S(1)} %get-tuple-element.8) | data formatting | bytes 1048576
  52.1 0.6 %copy.9 = f32[2,8,4,2,32]{4,3,2,1,0:T(2,128)} copy(f32[2,8,4,2,32]{4,3,2,1,0:T(2,128)S(1)} %bitcast.4) | data formatting | bytes 32768
Async XLA Ops:
  0.6 0.7 %copy-start.3 = (s32[512]{0:T(512)S(1)}, s32[512]{0:T(512)}, u32[]{:S(2)}) copy-start(s32[512]{0:T(512)} %param.7) | copy-start | bytes 6148
  1.3 1.2 %copy-start = (s32[512,512]{1,0:T(8,128)S(1)}, s32[512,512]{1,0:T(8,128)}, u32[]{:S(2)}) copy-start(s32[512,512]{1,0:T(8,128)} %phase.1) | copy-start | bytes 3145732
  2.5 1.0 %copy-start.1 = (bf16[2,8,2,32,256]{4,3,2,1,0:T(8,128)(2,1)S(1)}, bf16[2,8,2,32,256]{4,3,2,1,0:T(8,128)(2,1)}, u32[]{:S(2)}) copy-start(bf16[2,8,2,32,256]{4,3,2,1,0:T(8,128)(2,1)} %volt.1) | copy-start | bytes 1572868
  3.6 0.8 %copy-start.2 = (s32[2,8,4,2,32]{4,3,2,1,0:T(2,128)S(1)}, s32[2,8,4,2,32]{4,3,2,1,0:T(2,128)}, u32[]{:S(2)}) copy-start(s32[2,8,4,2,32]{4,3,2,1,0:T(2,128)} %param.5) | copy-start | bytes 49156

commit v2 on v1

v2 whole, which is shorter than its diff:
```python
import functools

import jax
import jax.numpy as jnp
from jax import lax
from jax.experimental import pallas as pl
from jax.experimental.pallas import tpu as pltpu
from jax.sharding import PartitionSpec as P

STATIONS = 512
CHANNELS = 32
ITERS = 3
PHASES = 1024
TIME = 512
RANK = 4
GROUP = 16
QUARTERS = 4

MESH = pl.DeviceIdType.MESH

COS_TERMS = (
    0.9999999998855527,
    -4.934802185863431,
    4.058711817242859,
    -1.3352602861671086,
    0.23532082553812417,
    -0.025785808775470303,
    0.0019043289643584185,
    -8.86909374720357e-05,
)
SIN_TERMS = (
    3.141592653568331,
    -5.167712777297557,
    2.5501639819324518,
    -0.599264064211247,
    0.0821440508162118,
    -0.007366486943808629,
    0.000461586777512204,
    -1.8944663042615234e-05,
)


def horner(terms, scale, v):
    total = jnp.full_like(v, terms[-1] * scale)
    for term in terms[-2::-1]:
        total = total * v + jnp.float32(term * scale)
    return total


def three_parts(value):
    high = value.astype(jnp.bfloat16)
    rest = value - high.astype(jnp.float32)
    middle = rest.astype(jnp.bfloat16)
    low = (rest - middle.astype(jnp.float32)).astype(jnp.bfloat16)
    return high, middle, low


def sum_of_three(rows):
    return rows[0:8] + (rows[8:16] + rows[16:24])


def half_swap(rows):
    return pltpu.roll(rows, 4, 0)


def exchange(
    volt,
    seed_hbm,
    phase,
    delay_hbm,
    arrived,
    rescale,
    basis_in,
    local_x,
    seed,
    phases,
    delay,
    field,
    first_out,
    first_in,
    image,
    weights,
    stage,
    power_out,
    power_in,
    power_two,
    basis_out,
    local_sem,
    send_x,
    recv_x,
    send_first,
    recv_first,
    send_image,
    recv_image,
    send_basis,
    recv_basis,
    send_power,
    recv_power,
    send_two,
    recv_two,
    send_beam,
    recv_beam,
):
    core = lax.axis_index("tm")
    me = lax.axis_index("station")
    plane = lax.axis_index("channel")
    mine = me // 2
    half = me % 2
    twin = me + 1 - 2 * half
    quarter = core * 2 + half

    def partner(step):
        across = (step // 4 + 2) % 4
        along = (step % 4 + 2) % 4
        row = (me // 4 + across) % 4
        column = (me % 4 + along) % 4
        return row * 4 + column

    def everyone(start):
        lax.fori_loop(0, 10, lambda step, carry: start(step) or carry, 0)
        lax.fori_loop(11, GROUP, lambda step, carry: start(step) or carry, 0)

    loads = [
        pltpu.make_async_copy(
            volt.at[part, :, :, :, pl.ds(side * 128, 128)],
            local_x.at[:, side, :, :, pl.ds(part * 128, 128)],
            local_sem.at[part * 2 + side],
        )
        for part in range(2)
        for side in range(2)
    ]
    loads.append(pltpu.make_async_copy(seed_hbm, seed, local_sem.at[4]))
    loads.append(pltpu.make_async_copy(phase, phases, local_sem.at[5]))
    loads.append(pltpu.make_async_copy(delay_hbm, delay, local_sem.at[6]))

    barrier = pltpu.get_barrier_semaphore()
    three = (
        {"tm": 1 - core, "station": twin},
        {"station": twin},
        {"tm": 1 - core},
    )
    seven = [{"channel": (plane + 2) % 4}, {"tm": 1 - core, "channel": (plane + 2) % 4}]
    for step in (1, 3):
        other = (plane + step) % 4
        seven.append({"channel": other})
        seven.append({"tm": 1 - core, "channel": other})
    seven.append({"tm": 1 - core})

    def greet(peer):
        pl.semaphore_signal(barrier, inc=1, device_id=peer, device_id_type=MESH)

    everyone(lambda step: greet({"station": partner(step)}))
    for peer in seven:
        greet(peer)
    greet(three[0])
    for load in loads:
        load.start()
    for load in loads[:4]:
        load.wait()
    pl.semaphore_wait(barrier, GROUP - 1 + len(seven) + 1)

    def x_copy(step, peer, slot):
        return pltpu.make_async_remote_copy(
            src_ref=local_x.at[peer // 2, peer % 2],
            dst_ref=field.at[slot],
            send_sem=send_x.at[step],
            recv_sem=recv_x.at[slot],
            device_id={"station": peer},
            device_id_type=MESH,
        )

    everyone(lambda step: x_copy(step, partner(step), me).start())
    own_x = pltpu.make_async_copy(local_x.at[mine, half], field.at[me], local_sem.at[7])
    own_x.start()

    row = lax.broadcasted_iota(jnp.int32, (8, 128), 0)
    upper = jnp.where(row < 4, 1.0, -1.0).astype(jnp.float32)

    loads[4].wait()
    for c in range(8):
        left = []
        for p in range(2):
            real_s = seed[0, c, pl.ds(p, 4, stride=2), :].astype(jnp.float32)
            imag_s = seed[1, c, pl.ds(p, 4, stride=2), :].astype(jnp.float32)
            left.append(jnp.concatenate([real_s, imag_s], axis=0))
        left = jnp.concatenate(left, axis=1).astype(jnp.bfloat16)
        for side in range(2):
            right = local_x[c, side].reshape(64, 256)
            rows = jnp.dot(left, right, preferred_element_type=jnp.float32)
            first_out[2 * c + side] = half_swap(rows[:, 128:256]) + upper * rows[:, 0:128]

    def first_copy(step, peer, slot):
        return pltpu.make_async_remote_copy(
            src_ref=first_out.at[peer],
            dst_ref=first_in.at[slot],
            send_sem=send_first.at[step],
            recv_sem=recv_first.at[slot],
            device_id={"station": peer},
            device_id_type=MESH,
        )

    everyone(lambda step: first_copy(step, partner(step), me).start())
    first_in[me] = first_out[me]

    loads[5].wait()
    loads[6].wait()
    number = plane * 8 + mine + 1
    norming = STATIONS**-0.5

    def weight_rows(block, carry):
        rows = pl.ds(pl.multiple_of(block * 32, 32), 32)
        index = (phases[rows, :] + delay[...]) * number
        wrapped = (index + PHASES // 2) & (PHASES - 1)
        u = (wrapped - PHASES // 2).astype(jnp.float32) * jnp.float32(2.0 / PHASES)
        v = u * u
        weights[0, rows, :] = horner(COS_TERMS, norming, v).astype(jnp.bfloat16)
        weights[1, rows, :] = (u * horner(SIN_TERMS, -norming, v)).astype(jnp.bfloat16)
        return carry

    lax.fori_loop(0, 16, weight_rows, 0)

    def arrive(step):
        source = partner(step)
        first_copy(step, source, source).wait_recv()
        x_copy(step, source, source).wait_recv()

    everyone(arrive)
    own_x.wait()

    def turned(c8):
        return jnp.concatenate([c8, half_swap(c8) * upper], axis=1)

    def apply_field(c8):
        left = jnp.concatenate(three_parts(turned(c8)), axis=0)
        right = field[...].reshape(1024, 256)
        rows = lax.dot_general(left, right, (((1,), (1,)), ((), ())), preferred_element_type=jnp.float32)
        return sum_of_three(rows)

    def coefficients(h8):
        left = jnp.concatenate(three_parts(h8), axis=0)
        rows = jnp.dot(left, field[...].reshape(1024, 256), preferred_element_type=jnp.float32)
        rows = sum_of_three(rows)
        return rows[:, 0:128] - upper * half_swap(rows[:, 128:256])

    def factor(h8):
        shifted = []
        for shift in range(4):
            moved = h8 * (pltpu.roll(h8, shift, 0) if shift else h8)
            lanes = moved[:, 0:128]
            for block in range(1, 8):
                lanes = lanes + moved[:, block * 128 : (block + 1) * 128]
            dots = jnp.broadcast_to(jnp.sum(lanes, axis=1, keepdims=True), (8, 128))
            swapped = half_swap(dots)
            shifted.append((dots + swapped, dots - swapped))

        def pick(rows, at):
            return jnp.broadcast_to(rows[at : at + 1, :], (8, 128))

        low = {}
        inverse = {}
        for column in range(RANK):
            diagonal = pick(shifted[0][0], column)
            for middle in range(column):
                re, im = low[column, middle]
                diagonal = diagonal - (re * re + im * im)
            inverse[column] = lax.rsqrt(diagonal)
            for at in range(column + 1, RANK):
                distance = at - column
                re = pick(shifted[distance][0], at)
                im = pick(shifted[4 - distance][1], column)
                for middle in range(column):
                    a_re, a_im = low[at, middle]
                    b_re, b_im = low[column, middle]
                    re = re - (a_re * b_re + a_im * b_im)
                    im = im - (a_im * b_re - a_re * b_im)
                low[at, column] = (re * inverse[column], im * inverse[column])
        return low, inverse

    def solve(low, inverse, rows):
        width = rows.shape[1]
        repeat = width // 128

        def wide(value):
            return value if repeat == 1 else jnp.concatenate([value] * repeat, axis=1)

        done = []
        for at in range(RANK):
            re = jnp.broadcast_to(rows[at : at + 1, :], (8, width))
            im = jnp.broadcast_to(rows[at + 4 : at + 5, :], (8, width))
            for middle in range(at):
                l_re, l_im = low[at, middle]
                l_re, l_im = wide(l_re), wide(l_im)
                d_re, d_im = done[middle]
                re = re - (l_re * d_re - l_im * d_im)
                im = im - (l_re * d_im + l_im * d_re)
            scale = wide(inverse[at])
            done.append((re * scale, im * scale))
        at_row = lax.broadcasted_iota(jnp.int32, (8, width), 0)
        total = done[3][1]
        for at in range(RANK):
            total = jnp.where(at_row == at, done[at][0], total)
            if at < 3:
                total = jnp.where(at_row == at + 4, done[at][1], total)
        return total

    coefficient = first_in[0]
    for station in range(1, GROUP):
        coefficient = coefficient + first_in[station]

    image_copies = []
    for iteration in range(ITERS):
        image[iteration, quarter] = apply_field(coefficient)
        for at, peer in enumerate(three):
            copy = pltpu.make_async_remote_copy(
                src_ref=image.at[iteration, quarter],
                dst_ref=image.at[iteration, quarter],
                send_sem=send_image.at[iteration, at],
                recv_sem=recv_image.at[iteration, at],
                device_id=peer,
                device_id_type=MESH,
            )
            copy.start()
            image_copies.append(copy)
        for copy in image_copies[-3:]:
            copy.wait_recv()
        summed = (image[iteration, 0] + image[iteration, 1]) + (image[iteration, 2] + image[iteration, 3])
        raw = coefficients(summed)
        low, inverse = factor(summed)
        coefficient = solve(low, inverse, raw)
    basis = solve(low, inverse, summed)

    for block in range(8):
        lanes = basis[:, block * 128 : (block + 1) * 128] * upper
        basis_out[2 * block] = lanes
        basis_out[2 * block + 1] = pltpu.roll(lanes, 64, 1)

    def basis_copy(step, slot, peer):
        return pltpu.make_async_remote_copy(
            src_ref=basis_out.at[peer],
            dst_ref=basis_in.at[slot],
            send_sem=send_basis.at[step],
            recv_sem=recv_basis.at[slot],
            device_id={"station": peer},
            device_id_type=MESH,
        )

    def basis_start(step):
        peer = partner(step)

        @pl.when(peer // 8 == half)
        def _():
            basis_copy(step, mine, peer).start()

    def six(parts, which):
        return jnp.concatenate([parts[at] for at in which], axis=0)

    left = six(three_parts(basis), (0, 0, 1, 0, 1, 2))
    right = six(three_parts(turned(coefficient)), (0, 1, 0, 2, 1, 0))
    removed = lax.dot_general(left, right, (((0,), (0,)), ((), ())), preferred_element_type=jnp.float32)
    cleaned = field[...].reshape(1024, 256).astype(jnp.float32) - removed
    cleaned = cleaned.astype(jnp.bfloat16).reshape(GROUP, 2, 32, 256)
    lane_group = lax.broadcasted_iota(jnp.int32, (8, 128), 1) // 16
    compact = [jnp.zeros((8, 128), jnp.float32) for _ in range(GROUP)]
    for p in range(2):
        ours = cleaned[:, p].reshape(512, 256)
        on_real = jnp.dot(weights[0], ours, preferred_element_type=jnp.float32)
        on_imag = jnp.dot(weights[1], ours, preferred_element_type=jnp.float32)
        real_b = on_real[:, 0:128] - on_imag[:, 128:256]
        imag_b = on_real[:, 128:256] + on_imag[:, 0:128]
        squares = jnp.sum(real_b * real_b + imag_b * imag_b, axis=1, keepdims=True)
        for station in range(GROUP):
            rows = slice(station * 32, (station + 1) * 32)
            stage[station, 0, p] = real_b[rows].astype(jnp.bfloat16)
            stage[station, 1, p] = imag_b[rows].astype(jnp.bfloat16)
            for block in range(4):
                at = station * 32 + block * 8
                compact[station] = jnp.where(
                    lane_group == p * 4 + block,
                    jnp.broadcast_to(squares[at : at + 8], (8, 128)),
                    compact[station],
                )
    for station in range(GROUP):
        power_out[station] = compact[station]

    def power_copy(step, peer, slot):
        return pltpu.make_async_remote_copy(
            src_ref=power_out.at[peer],
            dst_ref=power_in.at[slot],
            send_sem=send_power.at[step],
            recv_sem=recv_power.at[slot],
            device_id={"station": peer},
            device_id_type=MESH,
        )

    def beam_copy(step, peer, slot):
        return pltpu.make_async_remote_copy(
            src_ref=stage.at[peer],
            dst_ref=arrived.at[slot],
            send_sem=send_beam.at[step],
            recv_sem=recv_beam.at[slot],
            device_id={"station": peer},
            device_id_type=MESH,
        )

    everyone(lambda step: power_copy(step, partner(step), me).start())
    everyone(lambda step: beam_copy(step, partner(step), me).start())
    power_in[me] = power_out[me]
    own_beam = pltpu.make_async_copy(stage.at[me], arrived.at[me], local_sem.at[8])
    own_beam.start()
    everyone(basis_start)

    @pl.when(me // 8 == half)
    def _():
        copy = pltpu.make_async_copy(basis_out.at[me], basis_in.at[mine], local_sem.at[9])
        copy.start()
        copy.wait()

    def power_arrive(step):
        source = partner(step)
        power_copy(step, source, source).wait_recv()

    everyone(power_arrive)
    power = power_in[0]
    for station in range(1, GROUP):
        power = power + power_in[station]
    slot = plane * 2 + core
    power_two[slot] = power
    two_copies = []
    for at, peer in enumerate(seven):
        copy = pltpu.make_async_remote_copy(
            src_ref=power_two.at[slot],
            dst_ref=power_two.at[slot],
            send_sem=send_two.at[at],
            recv_sem=recv_two.at[at],
            device_id=peer,
            device_id_type=MESH,
        )
        copy.start()
        two_copies.append(copy)

    def drain(step):
        peer = partner(step)
        x_copy(step, peer, me).wait_send()
        first_copy(step, peer, me).wait_send()
        power_copy(step, peer, me).wait_send()

        @pl.when(peer // 8 == half)
        def _():
            basis_copy(step, mine, peer).wait_send()

    everyone(drain)
    for copy in image_copies:
        copy.wait_send()

    for copy in two_copies:
        copy.wait_recv()
    power = power_two[0]
    for at in range(1, 8):
        power = power + power_two[at]
    rescale[...] = lax.rsqrt(power / (CHANNELS * TIME) + 1e-06)

    for c in range(8):

        @pl.when(2 * c + me // 8 != me)
        def _():
            basis_copy(0, c, 2 * c + me // 8).wait_recv()

    def beam_arrive(step):
        source = partner(step)
        beam_copy(step, source, source).wait_recv()
        beam_copy(step, source, me).wait_send()

    everyone(beam_arrive)
    own_beam.wait()
    for copy in two_copies:
        copy.wait_send()


def normalise(arrived, rescale, basis, out, sub_hbm, result, sub, sem):
    scales = []
    for p in range(2):
        rows = []
        for block in range(4):
            lane = (p * 4 + block) * 16
            rows.append(jnp.broadcast_to(rescale[:, lane : lane + 1], (8, 128)))
        scales.append(jnp.concatenate(rows, axis=0))
    copies = []
    for c in range(8):
        for side in range(2):
            for part in range(2):
                for p in range(2):
                    value = arrived[2 * c + side, part, p].astype(jnp.float32) * scales[p]
                    result[part, c, p, :, side * 128 : (side + 1) * 128] = value.astype(jnp.bfloat16)
        copy = pltpu.make_async_copy(result.at[:, c], out.at[:, c], sem.at[c])
        copy.start()
        copies.append(copy)
    for c in range(8):
        for p in range(2):
            for part in range(2):
                at = part * 4
                sub[part, c, pl.ds(p, 4, stride=2), :] = basis[c, at : at + 4, p * 32 : (p + 1) * 32]
    copy = pltpu.make_async_copy(sub, sub_hbm, sem.at[8])
    copy.start()
    copies.append(copy)
    for copy in copies:
        copy.wait()


def body(voltages, start_seed, beam_phase, station_delay):
    vmem = pl.BlockSpec(memory_space=pltpu.VMEM)
    hbm = pl.BlockSpec(memory_space=pltpu.MemorySpace.HBM)
    anywhere = pl.BlockSpec(memory_space=pl.ANY)
    dma = pltpu.SemaphoreType.DMA
    f32, bf16 = jnp.float32, jnp.bfloat16
    def kept(value):
        return pltpu.with_memory_space_constraint(value, pltpu.MemorySpace.HBM)

    operands = (
        voltages,
        start_seed.reshape(2, 8, 8, 32),
        beam_phase,
        station_delay.reshape(1, STATIONS),
    )
    arrived, rescale, basis = pl.pallas_call(
        exchange,
        out_shape=(
            jax.ShapeDtypeStruct((16, 2, 2, 32, 128), bf16),
            jax.ShapeDtypeStruct((8, 128), f32),
            jax.ShapeDtypeStruct((8, 8, 128), f32),
        ),
        in_specs=[hbm] * 4,
        out_specs=(vmem, vmem, vmem),
        scratch_shapes=[
            pltpu.VMEM((8, 2, 2, 32, 256), bf16),
            pltpu.VMEM((2, 8, 8, 32), jnp.int32),
            pltpu.VMEM((512, 512), jnp.int32),
            pltpu.VMEM((1, 512), jnp.int32),
            pltpu.VMEM((GROUP, 2, 32, 256), bf16),
            pltpu.VMEM((GROUP, 8, 128), f32),
            pltpu.VMEM((GROUP, 8, 128), f32),
            pltpu.VMEM((ITERS, QUARTERS, 8, 1024), f32),
            pltpu.VMEM((2, 512, 512), bf16),
            pltpu.VMEM((GROUP, 2, 2, 32, 128), bf16),
            pltpu.VMEM((GROUP, 8, 128), f32),
            pltpu.VMEM((GROUP, 8, 128), f32),
            pltpu.VMEM((8, 8, 128), f32),
            pltpu.VMEM((GROUP, 8, 128), f32),
            dma((10,)),
            dma((16,)),
            dma((16,)),
            dma((16,)),
            dma((16,)),
            dma((ITERS, 3)),
            dma((ITERS, 3)),
            dma((16,)),
            dma((8,)),
            dma((16,)),
            dma((16,)),
            dma((7,)),
            dma((7,)),
            dma((16,)),
            dma((16,)),
        ],
        compiler_params=pltpu.CompilerParams(
            collective_id=0, has_side_effects=True, vmem_limit_bytes=40 * 1024 * 1024
        ),
    )(*map(kept, operands))
    beam_output, subspace = pl.pallas_call(
        normalise,
        out_shape=(
            jax.ShapeDtypeStruct((2, 8, 2, 32, 256), bf16),
            jax.ShapeDtypeStruct((2, 8, 8, 32), f32),
        ),
        in_specs=[vmem] * 3,
        out_specs=(anywhere, anywhere),
        scratch_shapes=[
            pltpu.VMEM((2, 8, 2, 32, 256), bf16),
            pltpu.VMEM((2, 8, 8, 32), f32),
            dma((9,)),
        ],
        compiler_params=pltpu.CompilerParams(vmem_limit_bytes=40 * 1024 * 1024),
    )(arrived, rescale, basis)
    return beam_output, subspace.reshape(2, 8, 4, 2, 32)


def solution(mesh):
    in_specs = (
        P(None, "channel", None, "station", "tm"),
        P(None, "channel", None, None, "station"),
        P(),
        P(),
    )
    out_specs = (
        P(None, "channel", None, "station", "tm"),
        P(None, "channel", None, None, "station"),
    )
    return jax.shard_map(body, mesh=mesh, in_specs=in_specs, out_specs=out_specs, check_vma=False)
```

time: 53 us -> 44.1 us (0.83)
  local copies, waits for them, and re-layouts: 5.2 us -> 0 us
  Pallas kernels: 46.9 us -> 43.3 us
    unnamed x10 -> x0, local copies, waits for them, and re-layouts: 5.2 us -> none
    pallas_call x1 -> x2, Pallas kernels: 46.9 us -> 43.3 us  [the longest x1 42.3 us: body(): pl.pallas_call(exchange, out_shape=(jax.ShapeDtypeStruct((16, 2, 2, 32, 1...]
where the time goes in v2:
time: 44.1 us; the launch traced here: 44 us
  Pallas kernels  43.3 us (98%)
  between operations  0.64 us (1%)
    pallas_call x1, Pallas kernels, body(): pl.pallas_call(exchange, out_shape=(jax.ShapeDtypeStruct((16, 2, 2, 32, 1...  42.3 us
    pallas_call x1, Pallas kernels, body(): pl.pallas_call(normalise, out_shape=(jax.ShapeDtypeStruct((2, 8, 2, 32, 2...  1.03 us

profile of v2, /device:TPU:1, one launch (start us, length us, event | category | flops | bytes accessed | tf_op | source)
XLA Modules:
  0.0 44.0 jit_solution(9188769023780824123)
XLA Ops:
  0.6 42.3 %shard_map.59 = (bf16[16,2,2,32,128]{4,3,2,1,0:T(8,128)(2,1)S(1)}, f32[8,128]{1,0:T(8,128)S(1)}, f32[8,8,128]{2,1,0:T(8,128)S(1)}) custom-call(bf16[2,8,2,32,256]{4,3,2,1,0:T(8,128)(2,1)} %volt.1, s32[2,8,8,32]{3,2,1,0:T(8,128)} %bitcast.3, s32[512,512]{1,0:T(8,128)} %phase.1, s32[1,512]{1,0:T(1,128)} %bitcast.4), custom_call_target="tpu_custom_call" | custom-call | tf_op jit(solution)/shard_map/pallas_call | solution.py:524
  42.9 1.0 %shard_map.60 = (bf16[2,8,2,32,256]{4,3,2,1,0:T(8,128)(2,1)}, f32[2,8,8,32]{3,2,1,0:T(8,128)}) custom-call(bf16[16,2,2,32,128]{4,3,2,1,0:T(8,128)(2,1)S(1)} %get-tuple-element.7.arrived, f32[8,128]{1,0:T(8,128)S(1)} %get-tuple-element.8.rescale, f32[8,8,128]{2,1,0:T(8,128)S(1)} %get-tuple-element.9.basis), custom_call_target="tpu_custom_call" | custom-call | tf_op jit(solution)/shard_map/pallas_call | solution.py:568

commit v3 on v2

--- a/solution.py
+++ b/solution.py
@@ -37,6 +37,25 @@
     -0.007366486943808629,
     0.000461586777512204,
     -1.8944663042615234e-05,
+)
+
+
+FARTHEST_FIRST = (
+    (2, 2),
+    (2, 1),
+    (2, 3),
+    (1, 2),
+    (3, 2),
+    (1, 1),
+    (3, 3),
+    (1, 3),
+    (3, 1),
+    (2, 0),
+    (0, 2),
+    (1, 0),
+    (3, 0),
+    (0, 1),
+    (0, 3),
 )
 
 
@@ -109,16 +128,19 @@
     twin = me + 1 - 2 * half
     quarter = core * 2 + half
 
-    def partner(step):
-        across = (step // 4 + 2) % 4
-        along = (step % 4 + 2) % 4
+    others = []
+    for across, along in FARTHEST_FIRST:
         row = (me // 4 + across) % 4
         column = (me % 4 + along) % 4
-        return row * 4 + column
+        others.append(row * 4 + column)
 
     def everyone(start):
-        lax.fori_loop(0, 10, lambda step, carry: start(step) or carry, 0)
-        lax.fori_loop(11, GROUP, lambda step, carry: start(step) or carry, 0)
+        for peer in others:
+            start(peer)
+
+    def together(buffer, sem):
+        part = buffer.at[pl.ds(0, GROUP - 1)]
+        return pltpu.make_async_copy(part, part, sem)
 
     loads = [
         pltpu.make_async_copy(
@@ -149,34 +171,17 @@
     def greet(peer):
         pl.semaphore_signal(barrier, inc=1, device_id=peer, device_id_type=MESH)
 
-    everyone(lambda step: greet({"station": partner(step)}))
+    everyone(lambda peer: greet({"station": peer}))
     for peer in seven:
         greet(peer)
     greet(three[0])
     for load in loads:
         load.start()
-    for load in loads[:4]:
-        load.wait()
-    pl.semaphore_wait(barrier, GROUP - 1 + len(seven) + 1)
-
-    def x_copy(step, peer, slot):
-        return pltpu.make_async_remote_copy(
-            src_ref=local_x.at[peer // 2, peer % 2],
-            dst_ref=field.at[slot],
-            send_sem=send_x.at[step],
-            recv_sem=recv_x.at[slot],
-            device_id={"station": peer},
-            device_id_type=MESH,
-        )
-
-    everyone(lambda step: x_copy(step, partner(step), me).start())
-    own_x = pltpu.make_async_copy(local_x.at[mine, half], field.at[me], local_sem.at[7])
-    own_x.start()
-
     row = lax.broadcasted_iota(jnp.int32, (8, 128), 0)
     upper = jnp.where(row < 4, 1.0, -1.0).astype(jnp.float32)
 
-    loads[4].wait()
+    for load in loads[:5]:
+        load.wait()
     for c in range(8):
         left = []
         for p in range(2):
@@ -189,17 +194,32 @@
             rows = jnp.dot(left, right, preferred_element_type=jnp.float32)
             first_out[2 * c + side] = half_swap(rows[:, 128:256]) + upper * rows[:, 0:128]
 
-    def first_copy(step, peer, slot):
+    pl.semaphore_wait(barrier, GROUP - 1 + len(seven) + 1)
+
+    def first_copy(peer):
         return pltpu.make_async_remote_copy(
             src_ref=first_out.at[peer],
-            dst_ref=first_in.at[slot],
-            send_sem=send_first.at[step],
-            recv_sem=recv_first.at[slot],
+            dst_ref=first_in.at[me],
+            send_sem=send_first,
+            recv_sem=recv_first,
             device_id={"station": peer},
             device_id_type=MESH,
         )
 
-    everyone(lambda step: first_copy(step, partner(step), me).start())
+    everyone(lambda peer: first_copy(peer).start())
+    def x_copy(peer):
+        return pltpu.make_async_remote_copy(
+            src_ref=local_x.at[peer // 2, peer % 2],
+            dst_ref=field.at[me],
+            send_sem=send_x,
+            recv_sem=recv_x,
+            device_id={"station": peer},
+            device_id_type=MESH,
+        )
+
+    everyone(lambda peer: x_copy(peer).start())
+    own_x = pltpu.make_async_copy(local_x.at[mine, half], field.at[me], local_sem.at[7])
+    own_x.start()
     first_in[me] = first_out[me]
 
     loads[5].wait()
@@ -219,12 +239,8 @@
 
     lax.fori_loop(0, 16, weight_rows, 0)
 
-    def arrive(step):
-        source = partner(step)
-        first_copy(step, source, source).wait_recv()
-        x_copy(step, source, source).wait_recv()
-
-    everyone(arrive)
+    together(first_in, recv_first).wait()
+    together(field, recv_x).wait()
     own_x.wait()
 
     def turned(c8):
@@ -334,22 +350,23 @@
         basis_out[2 * block] = lanes
         basis_out[2 * block + 1] = pltpu.roll(lanes, 64, 1)
 
-    def basis_copy(step, slot, peer):
+    def basis_copy(peer, slot):
         return pltpu.make_async_remote_copy(
             src_ref=basis_out.at[peer],
             dst_ref=basis_in.at[slot],
-            send_sem=send_basis.at[step],
+            send_sem=send_basis.at[peer],
             recv_sem=recv_basis.at[slot],
             device_id={"station": peer},
             device_id_type=MESH,
         )
 
-    def basis_start(step):
-        peer = partner(step)
-
-        @pl.when(peer // 8 == half)
-        def _():
-            basis_copy(step, mine, peer).start()
+    def served(start):
+        for inner in range(8):
+            peer = half * 8 + inner
+
+            @pl.when(peer != me)
+            def _():
+                start(basis_copy(peer, mine))
 
     def six(parts, which):
         return jnp.concatenate([parts[at] for at in which], axis=0)
@@ -382,32 +399,32 @@
     for station in range(GROUP):
         power_out[station] = compact[station]
 
-    def power_copy(step, peer, slot):
+    def power_copy(peer):
         return pltpu.make_async_remote_copy(
             src_ref=power_out.at[peer],
-            dst_ref=power_in.at[slot],
-            send_sem=send_power.at[step],
-            recv_sem=recv_power.at[slot],
+            dst_ref=power_in.at[me],
+            send_sem=send_power,
+            recv_sem=recv_power,
             device_id={"station": peer},
             device_id_type=MESH,
         )
 
-    def beam_copy(step, peer, slot):
+    def beam_copy(peer):
         return pltpu.make_async_remote_copy(
             src_ref=stage.at[peer],
-            dst_ref=arrived.at[slot],
-            send_sem=send_beam.at[step],
-            recv_sem=recv_beam.at[slot],
+            dst_ref=arrived.at[me],
+            send_sem=send_beam,
+            recv_sem=recv_beam,
             device_id={"station": peer},
             device_id_type=MESH,
         )
 
-    everyone(lambda step: power_copy(step, partner(step), me).start())
-    everyone(lambda step: beam_copy(step, partner(step), me).start())
+    everyone(lambda peer: power_copy(peer).start())
+    everyone(lambda peer: beam_copy(peer).start())
     power_in[me] = power_out[me]
     own_beam = pltpu.make_async_copy(stage.at[me], arrived.at[me], local_sem.at[8])
     own_beam.start()
-    everyone(basis_start)
+    served(lambda copy: copy.start())
 
     @pl.when(me // 8 == half)
     def _():
@@ -415,11 +432,7 @@
         copy.start()
         copy.wait()
 
-    def power_arrive(step):
-        source = partner(step)
-        power_copy(step, source, source).wait_recv()
-
-    everyone(power_arrive)
+    together(power_in, recv_power).wait()
     power = power_in[0]
     for station in range(1, GROUP):
         power = power + power_in[station]
@@ -438,19 +451,21 @@
         copy.start()
         two_copies.append(copy)
 
-    def drain(step):
-        peer = partner(step)
-        x_copy(step, peer, me).wait_send()
-        first_copy(step, peer, me).wait_send()
-        power_copy(step, peer, me).wait_send()
-
-        @pl.when(peer // 8 == half)
-        def _():
-            basis_copy(step, mine, peer).wait_send()
-
-    everyone(drain)
+    together(first_out, send_first).wait()
+    together(field, send_x).wait()
+    together(power_out, send_power).wait()
     for copy in image_copies:
         copy.wait_send()
+    served(lambda copy: copy.wait_send())
+    for c in range(8):
+
+        @pl.when(2 * c + me // 8 != me)
+        def _():
+            basis_copy(2 * c + me // 8, c).wait_recv()
+
+    together(stage, send_beam).wait()
+    together(arrived, recv_beam).wait()
+    own_beam.wait()
 
     for copy in two_copies:
         copy.wait_recv()
@@ -459,19 +474,6 @@
         power = power + power_two[at]
     rescale[...] = lax.rsqrt(power / (CHANNELS * TIME) + 1e-06)
 
-    for c in range(8):
-
-        @pl.when(2 * c + me // 8 != me)
-        def _():
-            basis_copy(0, c, 2 * c + me // 8).wait_recv()
-
-    def beam_arrive(step):
-        source = partner(step)
-        beam_copy(step, source, source).wait_recv()
-        beam_copy(step, source, me).wait_send()
-
-    everyone(beam_arrive)
-    own_beam.wait()
     for copy in two_copies:
         copy.wait_send()
 
@@ -546,20 +548,20 @@
             pltpu.VMEM((8, 8, 128), f32),
             pltpu.VMEM((GROUP, 8, 128), f32),
             dma((10,)),
-            dma((16,)),
-            dma((16,)),
-            dma((16,)),
-            dma((16,)),
+            dma(()),
+            dma(()),
+            dma(()),
+            dma(()),
             dma((ITERS, 3)),
             dma((ITERS, 3)),
             dma((16,)),
             dma((8,)),
-            dma((16,)),
-            dma((16,)),
+            dma(()),
+            dma(()),
             dma((7,)),
             dma((7,)),
-            dma((16,)),
-            dma((16,)),
+            dma(()),
+            dma(()),
         ],
         compiler_params=pltpu.CompilerParams(
             collective_id=0, has_side_effects=True, vmem_limit_bytes=40 * 1024 * 1024

time: 44.1 us -> 41.3 us (0.937)
  Pallas kernels: 43.3 us -> 40.6 us
    pallas_call x1, Pallas kernels: 42.3 us -> 39.5 us  [body(): pl.pallas_call(exchange, out_shape=(jax.ShapeDtypeStruct((16, 2, 2, 32, 1...]
where the time goes in v3:
time: 41.3 us; the launch traced here: 41.2 us
  Pallas kernels  40.6 us (98%)
  between operations  0.64 us (2%)
    pallas_call x1, Pallas kernels, body(): pl.pallas_call(exchange, out_shape=(jax.ShapeDtypeStruct((16, 2, 2, 32, 1...  39.5 us
    pallas_call x1, Pallas kernels, body(): pl.pallas_call(normalise, out_shape=(jax.ShapeDtypeStruct((2, 8, 2, 32, 2...  1.03 us

profile of v3, /device:TPU:1, one launch (start us, length us, event | category | flops | bytes accessed | tf_op | source)
XLA Modules:
  0.0 41.2 jit_solution(8455603435963548164)
XLA Ops:
  0.6 39.5 %shard_map.59 = (bf16[16,2,2,32,128]{4,3,2,1,0:T(8,128)(2,1)S(1)}, f32[8,128]{1,0:T(8,128)S(1)}, f32[8,8,128]{2,1,0:T(8,128)S(1)}) custom-call(bf16[2,8,2,32,256]{4,3,2,1,0:T(8,128)(2,1)} %volt.1, s32[2,8,8,32]{3,2,1,0:T(8,128)} %bitcast.3, s32[512,512]{1,0:T(8,128)} %phase.1, s32[1,512]{1,0:T(1,128)} %bitcast.4), custom_call_target="tpu_custom_call" | custom-call | tf_op jit(solution)/shard_map/pallas_call | solution.py:526
  40.2 1.0 %shard_map.60 = (bf16[2,8,2,32,256]{4,3,2,1,0:T(8,128)(2,1)}, f32[2,8,8,32]{3,2,1,0:T(8,128)}) custom-call(bf16[16,2,2,32,128]{4,3,2,1,0:T(8,128)(2,1)S(1)} %get-tuple-element.7.arrived, f32[8,128]{1,0:T(8,128)S(1)} %get-tuple-element.8.rescale, f32[8,8,128]{2,1,0:T(8,128)S(1)} %get-tuple-element.9.basis), custom_call_target="tpu_custom_call" | custom-call | tf_op jit(solution)/shard_map/pallas_call | solution.py:570

commit v4 on v3

--- a/solution.py
+++ b/solution.py
@@ -57,6 +57,7 @@
     (0, 1),
     (0, 3),
 )
+BEAM_TURNS = (0, 13, 1, 12, 2, 11, 3, 14, 4, 9, 10, 5, 6, 7, 8)
 
 
 def horner(terms, scale, v):
@@ -89,7 +90,7 @@
     delay_hbm,
     arrived,
     rescale,
-    basis_in,
+    power_in,
     local_x,
     seed,
     phases,
@@ -101,9 +102,7 @@
     weights,
     stage,
     power_out,
-    power_in,
     power_two,
-    basis_out,
     local_sem,
     send_x,
     recv_x,
@@ -111,8 +110,6 @@
     recv_first,
     send_image,
     recv_image,
-    send_basis,
-    recv_basis,
     send_power,
     recv_power,
     send_two,
@@ -345,29 +342,6 @@
         coefficient = solve(low, inverse, raw)
     basis = solve(low, inverse, summed)
 
-    for block in range(8):
-        lanes = basis[:, block * 128 : (block + 1) * 128] * upper
-        basis_out[2 * block] = lanes
-        basis_out[2 * block + 1] = pltpu.roll(lanes, 64, 1)
-
-    def basis_copy(peer, slot):
-        return pltpu.make_async_remote_copy(
-            src_ref=basis_out.at[peer],
-            dst_ref=basis_in.at[slot],
-            send_sem=send_basis.at[peer],
-            recv_sem=recv_basis.at[slot],
-            device_id={"station": peer},
-            device_id_type=MESH,
-        )
-
-    def served(start):
-        for inner in range(8):
-            peer = half * 8 + inner
-
-            @pl.when(peer != me)
-            def _():
-                start(basis_copy(peer, mine))
-
     def six(parts, which):
         return jnp.concatenate([parts[at] for at in which], axis=0)
 
@@ -376,8 +350,11 @@
     removed = lax.dot_general(left, right, (((0,), (0,)), ((), ())), preferred_element_type=jnp.float32)
     cleaned = field[...].reshape(1024, 256).astype(jnp.float32) - removed
     cleaned = cleaned.astype(jnp.bfloat16).reshape(GROUP, 2, 32, 256)
-    lane_group = lax.broadcasted_iota(jnp.int32, (8, 128), 1) // 16
-    compact = [jnp.zeros((8, 128), jnp.float32) for _ in range(GROUP)]
+    lane_group = lax.broadcasted_iota(jnp.int32, (8, 128), 1) // 8
+    compact = []
+    for block in range(8):
+        lanes = basis[:, block * 128 : (block + 1) * 128] * upper
+        compact += [pltpu.roll(lanes, 64, 1), lanes]
     for p in range(2):
         ours = cleaned[:, p].reshape(512, 256)
         on_real = jnp.dot(weights[0], ours, preferred_element_type=jnp.float32)
@@ -420,17 +397,11 @@
         )
 
     everyone(lambda peer: power_copy(peer).start())
-    everyone(lambda peer: beam_copy(peer).start())
+    for at in BEAM_TURNS:
+        beam_copy(others[at]).start()
     power_in[me] = power_out[me]
     own_beam = pltpu.make_async_copy(stage.at[me], arrived.at[me], local_sem.at[8])
     own_beam.start()
-    served(lambda copy: copy.start())
-
-    @pl.when(me // 8 == half)
-    def _():
-        copy = pltpu.make_async_copy(basis_out.at[me], basis_in.at[mine], local_sem.at[9])
-        copy.start()
-        copy.wait()
 
     together(power_in, recv_power).wait()
     power = power_in[0]
@@ -456,13 +427,6 @@
     together(power_out, send_power).wait()
     for copy in image_copies:
         copy.wait_send()
-    served(lambda copy: copy.wait_send())
-    for c in range(8):
-
-        @pl.when(2 * c + me // 8 != me)
-        def _():
-            basis_copy(2 * c + me // 8, c).wait_recv()
-
     together(stage, send_beam).wait()
     together(arrived, recv_beam).wait()
     own_beam.wait()
@@ -483,7 +447,7 @@
     for p in range(2):
         rows = []
         for block in range(4):
-            lane = (p * 4 + block) * 16
+            lane = (p * 4 + block) * 8
             rows.append(jnp.broadcast_to(rescale[:, lane : lane + 1], (8, 128)))
         scales.append(jnp.concatenate(rows, axis=0))
     copies = []
@@ -500,7 +464,7 @@
         for p in range(2):
             for part in range(2):
                 at = part * 4
-                sub[part, c, pl.ds(p, 4, stride=2), :] = basis[c, at : at + 4, p * 32 : (p + 1) * 32]
+                sub[part, c, pl.ds(p, 4, stride=2), :] = basis[2 * c, at : at + 4, 64 + p * 32 : 96 + p * 32]
     copy = pltpu.make_async_copy(sub, sub_hbm, sem.at[8])
     copy.start()
     copies.append(copy)
@@ -528,7 +492,7 @@
         out_shape=(
             jax.ShapeDtypeStruct((16, 2, 2, 32, 128), bf16),
             jax.ShapeDtypeStruct((8, 128), f32),
-            jax.ShapeDtypeStruct((8, 8, 128), f32),
+            jax.ShapeDtypeStruct((GROUP, 8, 128), f32),
         ),
         in_specs=[hbm] * 4,
         out_specs=(vmem, vmem, vmem),
@@ -544,9 +508,7 @@
             pltpu.VMEM((2, 512, 512), bf16),
             pltpu.VMEM((GROUP, 2, 2, 32, 128), bf16),
             pltpu.VMEM((GROUP, 8, 128), f32),
-            pltpu.VMEM((GROUP, 8, 128), f32),
             pltpu.VMEM((8, 8, 128), f32),
-            pltpu.VMEM((GROUP, 8, 128), f32),
             dma((10,)),
             dma(()),
             dma(()),
@@ -554,8 +516,6 @@
             dma(()),
             dma((ITERS, 3)),
             dma((ITERS, 3)),
-            dma((16,)),
-            dma((8,)),
             dma(()),
             dma(()),
             dma((7,)),

time: 41.3 us -> 40.3 us (0.976)
  Pallas kernels: 40.6 us -> 39.6 us
    pallas_call x1, Pallas kernels: 39.5 us -> 38.5 us  [body(): pl.pallas_call(exchange, out_shape=(jax.ShapeDtypeStruct((16, 2, 2, 32, 1...]
where the time goes in v4:
time: 40.3 us; the launch traced here: 40.2 us
  Pallas kernels  39.6 us (98%)
  between operations  0.64 us (2%)
    pallas_call x1, Pallas kernels, body(): pl.pallas_call(exchange, out_shape=(jax.ShapeDtypeStruct((16, 2, 2, 32, 1...  38.5 us
    pallas_call x1, Pallas kernels, body(): pl.pallas_call(normalise, out_shape=(jax.ShapeDtypeStruct((2, 8, 2, 32, 2...  1.03 us

profile of v4, /device:TPU:1, one launch (start us, length us, event | category | flops | bytes accessed | tf_op | source)
XLA Modules:
  0.0 40.2 jit_solution(9621060728581409892)
XLA Ops:
  0.6 38.5 %shard_map.59 = (bf16[16,2,2,32,128]{4,3,2,1,0:T(8,128)(2,1)S(1)}, f32[8,128]{1,0:T(8,128)S(1)}, f32[16,8,128]{2,1,0:T(8,128)S(1)}) custom-call(bf16[2,8,2,32,256]{4,3,2,1,0:T(8,128)(2,1)} %volt.1, s32[2,8,8,32]{3,2,1,0:T(8,128)} %bitcast.3, s32[512,512]{1,0:T(8,128)} %phase.1, s32[1,512]{1,0:T(1,128)} %bitcast.4), custom_call_target="tpu_custom_call" | custom-call | tf_op jit(solution)/shard_map/pallas_call | solution.py:490
  39.2 1.0 %shard_map.60 = (bf16[2,8,2,32,256]{4,3,2,1,0:T(8,128)(2,1)}, f32[2,8,8,32]{3,2,1,0:T(8,128)}) custom-call(bf16[16,2,2,32,128]{4,3,2,1,0:T(8,128)(2,1)S(1)} %get-tuple-element.7.arrived, f32[8,128]{1,0:T(8,128)S(1)} %get-tuple-element.8.rescale, f32[16,8,128]{2,1,0:T(8,128)S(1)} %get-tuple-element.9.basis), custom_call_target="tpu_custom_call" | custom-call | tf_op jit(solution)/shard_map/pallas_call | solution.py:530

commit v5 on v4

--- a/solution.py
+++ b/solution.py
@@ -189,7 +189,8 @@
         for side in range(2):
             right = local_x[c, side].reshape(64, 256)
             rows = jnp.dot(left, right, preferred_element_type=jnp.float32)
-            first_out[2 * c + side] = half_swap(rows[:, 128:256]) + upper * rows[:, 0:128]
+            share = half_swap(rows[:, 128:256]) + upper * rows[:, 0:128]
+            first_out[2 * c + side] = share.astype(jnp.bfloat16)
 
     pl.semaphore_wait(barrier, GROUP - 1 + len(seven) + 1)
 
@@ -203,7 +204,6 @@
             device_id_type=MESH,
         )
 
-    everyone(lambda peer: first_copy(peer).start())
     def x_copy(peer):
         return pltpu.make_async_remote_copy(
             src_ref=local_x.at[peer // 2, peer % 2],
@@ -214,7 +214,11 @@
             device_id_type=MESH,
         )
 
-    everyone(lambda peer: x_copy(peer).start())
+    for peer in others[:3]:
+        x_copy(peer).start()
+    everyone(lambda peer: first_copy(peer).start())
+    for peer in others[3:]:
+        x_copy(peer).start()
     own_x = pltpu.make_async_copy(local_x.at[mine, half], field.at[me], local_sem.at[7])
     own_x.start()
     first_in[me] = first_out[me]
@@ -316,9 +320,7 @@
                 total = jnp.where(at_row == at + 4, done[at][1], total)
         return total
 
-    coefficient = first_in[0]
-    for station in range(1, GROUP):
-        coefficient = coefficient + first_in[station]
+    coefficient = jnp.sum(first_in[...].astype(jnp.float32), axis=0)
 
     image_copies = []
     for iteration in range(ITERS):
@@ -502,8 +504,8 @@
             pltpu.VMEM((512, 512), jnp.int32),
             pltpu.VMEM((1, 512), jnp.int32),
             pltpu.VMEM((GROUP, 2, 32, 256), bf16),
-            pltpu.VMEM((GROUP, 8, 128), f32),
-            pltpu.VMEM((GROUP, 8, 128), f32),
+            pltpu.VMEM((GROUP, 8, 128), bf16),
+            pltpu.VMEM((GROUP, 8, 128), bf16),
             pltpu.VMEM((ITERS, QUARTERS, 8, 1024), f32),
             pltpu.VMEM((2, 512, 512), bf16),
             pltpu.VMEM((GROUP, 2, 2, 32, 128), bf16),

time: 40.3 us -> 39.9 us (0.990)
    pallas_call x1, Pallas kernels: 38.5 us -> 38.1 us  [body(): pl.pallas_call(exchange, out_shape=(jax.ShapeDtypeStruct((16, 2, 2, 32, 1...]
where the time goes in v5:
time: 39.9 us; the launch traced here: 39.8 us
  Pallas kernels  39.2 us (98%)
  between operations  0.64 us (2%)
    pallas_call x1, Pallas kernels, body(): pl.pallas_call(exchange, out_shape=(jax.ShapeDtypeStruct((16, 2, 2, 32, 1...  38.1 us
    pallas_call x1, Pallas kernels, body(): pl.pallas_call(normalise, out_shape=(jax.ShapeDtypeStruct((2, 8, 2, 32, 2...  1.03 us

profile of v5, /device:TPU:1, one launch (start us, length us, event | category | flops | bytes accessed | tf_op | source)
XLA Modules:
  0.0 39.8 jit_solution(8989115298053168203)
XLA Ops:
  0.6 38.1 %shard_map.59 = (bf16[16,2,2,32,128]{4,3,2,1,0:T(8,128)(2,1)S(1)}, f32[8,128]{1,0:T(8,128)S(1)}, f32[16,8,128]{2,1,0:T(8,128)S(1)}) custom-call(bf16[2,8,2,32,256]{4,3,2,1,0:T(8,128)(2,1)} %volt.1, s32[2,8,8,32]{3,2,1,0:T(8,128)} %bitcast.3, s32[512,512]{1,0:T(8,128)} %phase.1, s32[1,512]{1,0:T(1,128)} %bitcast.4), custom_call_target="tpu_custom_call" | custom-call | tf_op jit(solution)/shard_map/pallas_call | solution.py:492
  38.8 1.0 %shard_map.60 = (bf16[2,8,2,32,256]{4,3,2,1,0:T(8,128)(2,1)}, f32[2,8,8,32]{3,2,1,0:T(8,128)}) custom-call(bf16[16,2,2,32,128]{4,3,2,1,0:T(8,128)(2,1)S(1)} %get-tuple-element.7.arrived, f32[8,128]{1,0:T(8,128)S(1)} %get-tuple-element.8.rescale, f32[16,8,128]{2,1,0:T(8,128)S(1)} %get-tuple-element.9.basis), custom_call_target="tpu_custom_call" | custom-call | tf_op jit(solution)/shard_map/pallas_call | solution.py:532

commit v6 on v5

--- a/solution.py
+++ b/solution.py
@@ -90,7 +90,7 @@
     delay_hbm,
     arrived,
     rescale,
-    power_in,
+    sub,
     local_x,
     seed,
     phases,
@@ -102,6 +102,7 @@
     weights,
     stage,
     power_out,
+    power_in,
     power_two,
     local_sem,
     send_x,
@@ -424,6 +425,12 @@
         copy.start()
         two_copies.append(copy)
 
+    for c in range(8):
+        for p in range(2):
+            for part in range(2):
+                at = part * 4
+                sub[part, c, pl.ds(p, 4, stride=2), :] = power_in[2 * c, at : at + 4, 64 + p * 32 : 96 + p * 32]
+
     together(first_out, send_first).wait()
     together(field, send_x).wait()
     together(power_out, send_power).wait()
@@ -444,7 +451,10 @@
         copy.wait_send()
 
 
-def normalise(arrived, rescale, basis, out, sub_hbm, result, sub, sem):
+def normalise(arrived, rescale, sub, out, sub_hbm, result, sem):
+    copy = pltpu.make_async_copy(sub, sub_hbm, sem.at[8])
+    copy.start()
+    copies = [copy]
     scales = []
     for p in range(2):
         rows = []
@@ -452,7 +462,6 @@
             lane = (p * 4 + block) * 8
             rows.append(jnp.broadcast_to(rescale[:, lane : lane + 1], (8, 128)))
         scales.append(jnp.concatenate(rows, axis=0))
-    copies = []
     for c in range(8):
         for side in range(2):
             for part in range(2):
@@ -462,14 +471,6 @@
         copy = pltpu.make_async_copy(result.at[:, c], out.at[:, c], sem.at[c])
         copy.start()
         copies.append(copy)
-    for c in range(8):
-        for p in range(2):
-            for part in range(2):
-                at = part * 4
-                sub[part, c, pl.ds(p, 4, stride=2), :] = basis[2 * c, at : at + 4, 64 + p * 32 : 96 + p * 32]
-    copy = pltpu.make_async_copy(sub, sub_hbm, sem.at[8])
-    copy.start()
-    copies.append(copy)
     for copy in copies:
         copy.wait()
 
@@ -489,12 +490,12 @@
         beam_phase,
         station_delay.reshape(1, STATIONS),
     )
-    arrived, rescale, basis = pl.pallas_call(
+    arrived, rescale, sub = pl.pallas_call(
         exchange,
         out_shape=(
             jax.ShapeDtypeStruct((16, 2, 2, 32, 128), bf16),
             jax.ShapeDtypeStruct((8, 128), f32),
-            jax.ShapeDtypeStruct((GROUP, 8, 128), f32),
+            jax.ShapeDtypeStruct((2, 8, 8, 32), f32),
         ),
         in_specs=[hbm] * 4,
         out_specs=(vmem, vmem, vmem),
@@ -510,6 +511,7 @@
             pltpu.VMEM((2, 512, 512), bf16),
             pltpu.VMEM((GROUP, 2, 2, 32, 128), bf16),
             pltpu.VMEM((GROUP, 8, 128), f32),
+            pltpu.VMEM((GROUP, 8, 128), f32),
             pltpu.VMEM((8, 8, 128), f32),
             dma((10,)),
             dma(()),
@@ -539,11 +541,10 @@
         out_specs=(anywhere, anywhere),
         scratch_shapes=[
             pltpu.VMEM((2, 8, 2, 32, 256), bf16),
-            pltpu.VMEM((2, 8, 8, 32), f32),
             dma((9,)),
         ],
         compiler_params=pltpu.CompilerParams(vmem_limit_bytes=40 * 1024 * 1024),
-    )(arrived, rescale, basis)
+    )(arrived, rescale, sub)
     return beam_output, subspace.reshape(2, 8, 4, 2, 32)
 
 

time: 39.9 us -> 39.9 us (level)
  no operation moved by 1% of the time
where the time goes in v6:
time: 39.9 us; the launch traced here: 39.8 us
  Pallas kernels  39.1 us (98%)
  between operations  0.64 us (2%)
    pallas_call x1, Pallas kernels, body(): pl.pallas_call(exchange, out_shape=(jax.ShapeDtypeStruct((16, 2, 2, 32, 1...  38.1 us
    pallas_call x1, Pallas kernels, body(): pl.pallas_call(normalise, out_shape=(jax.ShapeDtypeStruct((2, 8, 2, 32, 2...  0.99 us

profile of v6, /device:TPU:1, one launch (start us, length us, event | category | flops | bytes accessed | tf_op | source)
XLA Modules:
  0.0 39.8 jit_solution(1725014326724016967)
XLA Ops:
  0.6 38.1 %shard_map.59 = (bf16[16,2,2,32,128]{4,3,2,1,0:T(8,128)(2,1)S(1)}, f32[8,128]{1,0:T(8,128)S(1)}, f32[2,8,8,32]{3,2,1,0:T(8,128)S(1)}) custom-call(bf16[2,8,2,32,256]{4,3,2,1,0:T(8,128)(2,1)} %volt.1, s32[2,8,8,32]{3,2,1,0:T(8,128)} %bitcast.3, s32[512,512]{1,0:T(8,128)} %phase.1, s32[1,512]{1,0:T(1,128)} %bitcast.4), custom_call_target="tpu_custom_call" | custom-call | tf_op jit(solution)/shard_map/pallas_call | solution.py:493
  38.8 1.0 %shard_map.60 = (bf16[2,8,2,32,256]{4,3,2,1,0:T(8,128)(2,1)}, f32[2,8,8,32]{3,2,1,0:T(8,128)}) custom-call(bf16[16,2,2,32,128]{4,3,2,1,0:T(8,128)(2,1)S(1)} %get-tuple-element.7.arrived, f32[8,128]{1,0:T(8,128)S(1)} %get-tuple-element.8.rescale, f32[2,8,8,32]{3,2,1,0:T(8,128)S(1)} %get-tuple-element.9.sub), custom_call_target="tpu_custom_call" | custom-call | tf_op jit(solution)/shard_map/pallas_call | solution.py:534

commit v7 on v5

--- a/solution.py
+++ b/solution.py
@@ -354,6 +354,7 @@
     cleaned = cleaned.astype(jnp.bfloat16).reshape(GROUP, 2, 32, 256)
     lane_group = lax.broadcasted_iota(jnp.int32, (8, 128), 1) // 8
     compact = []
+    kept_beams = []
     for block in range(8):
         lanes = basis[:, block * 128 : (block + 1) * 128] * upper
         compact += [pltpu.roll(lanes, 64, 1), lanes]
@@ -363,11 +364,10 @@
         on_imag = jnp.dot(weights[1], ours, preferred_element_type=jnp.float32)
         real_b = on_real[:, 0:128] - on_imag[:, 128:256]
         imag_b = on_real[:, 128:256] + on_imag[:, 0:128]
+        kept_beams.append((real_b, imag_b))
         squares = jnp.sum(real_b * real_b + imag_b * imag_b, axis=1, keepdims=True)
         for station in range(GROUP):
             rows = slice(station * 32, (station + 1) * 32)
-            stage[station, 0, p] = real_b[rows].astype(jnp.bfloat16)
-            stage[station, 1, p] = imag_b[rows].astype(jnp.bfloat16)
             for block in range(4):
                 at = station * 32 + block * 8
                 compact[station] = jnp.where(
@@ -399,6 +399,11 @@
         )
 
     everyone(lambda peer: power_copy(peer).start())
+    for p in range(2):
+        for station in range(GROUP):
+            rows = slice(station * 32, (station + 1) * 32)
+            for part in range(2):
+                stage[station, part, p] = kept_beams[p][part][rows].astype(jnp.bfloat16)
     for at in BEAM_TURNS:
         beam_copy(others[at]).start()
     power_in[me] = power_out[me]

time: 39.9 us -> 39.9 us (level)
  no operation moved by 1% of the time
where the time goes in v7:
time: 39.9 us; the launch traced here: 39.8 us
  Pallas kernels  39.2 us (98%)
  between operations  0.64 us (2%)
    pallas_call x1, Pallas kernels, body(): pl.pallas_call(exchange, out_shape=(jax.ShapeDtypeStruct((16, 2, 2, 32, 1...  38.1 us
    pallas_call x1, Pallas kernels, body(): pl.pallas_call(normalise, out_shape=(jax.ShapeDtypeStruct((2, 8, 2, 32, 2...  1.03 us

profile of v7, /device:TPU:1, one launch (start us, length us, event | category | flops | bytes accessed | tf_op | source)
XLA Modules:
  0.0 39.8 jit_solution(7218333924763860314)
XLA Ops:
  0.6 38.1 %shard_map.59 = (bf16[16,2,2,32,128]{4,3,2,1,0:T(8,128)(2,1)S(1)}, f32[8,128]{1,0:T(8,128)S(1)}, f32[16,8,128]{2,1,0:T(8,128)S(1)}) custom-call(bf16[2,8,2,32,256]{4,3,2,1,0:T(8,128)(2,1)} %volt.1, s32[2,8,8,32]{3,2,1,0:T(8,128)} %bitcast.3, s32[512,512]{1,0:T(8,128)} %phase.1, s32[1,512]{1,0:T(1,128)} %bitcast.4), custom_call_target="tpu_custom_call" | custom-call | tf_op jit(solution)/shard_map/pallas_call | solution.py:497
  38.8 1.0 %shard_map.60 = (bf16[2,8,2,32,256]{4,3,2,1,0:T(8,128)(2,1)}, f32[2,8,8,32]{3,2,1,0:T(8,128)}) custom-call(bf16[16,2,2,32,128]{4,3,2,1,0:T(8,128)(2,1)S(1)} %get-tuple-element.7.arrived, f32[8,128]{1,0:T(8,128)S(1)} %get-tuple-element.8.rescale, f32[16,8,128]{2,1,0:T(8,128)S(1)} %get-tuple-element.9.basis), custom_call_target="tpu_custom_call" | custom-call | tf_op jit(solution)/shard_map/pallas_call | solution.py:537
